TPU v7x, 512 devices: a whole 4x4x16 slice. The times are simulated.
512 devices in a mesh: ev: 8 (over y, x_hi), gx: 16 (over z), gy: 4 (over x_lo, core).
Axes of the slice: x: 4 (x_hi: 2, x_lo: 2; x = x_hi * 2 + x_lo), y: 4, z: 16, core: 2. Of those that a mesh axis runs over, the one named last changes fastest.
Arguments:
- forward_state: float32 [8, 9, 4, 256, 512], P('ev', None, None, 'gx', 'gy'), may hold values from -6 to 6
- adjoint_state: float32 [8, 9, 4, 256, 512], P('ev', None, None, 'gx', 'gy'), may hold values from -6 to 6
- first_lame_parameter: float32 [4, 256, 512], P(None, 'gx', 'gy'), may hold values from 0.5 to 2
- shear_stiffness: float32 [4, 256, 512], P(None, 'gx', 'gy'), may hold values from 0.5 to 1.5
- buoyancy: float32 [4, 256, 512], P(None, 'gx', 'gy'), may hold values from 0.5 to 1.5
- layer_mask: int32 [4, 256, 512], P(None, 'gx', 'gy'), may hold values 0 or 1
- layer_element: int32 [4, 256, 512], P(None, 'gx', 'gy'), may hold values from 0 to 511
- layer_forces: float32 [8, 3, 512], P('ev'), may hold values from -24 to 24
Outputs:
- forward_next: float32 [8, 9, 4, 256, 512], P('ev', None, None, 'gx', 'gy')
- kernels: float32 [3, 4, 256, 512], P(None, None, 'gx', 'gy')
All inputs are finite; a program needn't handle non-finite values. No bound on the sum of `layer_mask` on one device may be relied on, other than what follows from the above.
Results may differ from a plain program's by a relative error of at most 0.00002.
Values sent between devices are 32-bit elements; how exact they have to be, the bound alone decides.
No kernel may reach another device: no remote copies, remote signals or barrier semaphores. Data moves between devices by JAX's collectives and lax.ppermute only.
A program may use at most 64 MiB of HBM per device.

v0:
```python
import jax
import jax.numpy as jnp
from jax import lax
from jax.sharding import PartitionSpec as P

inner_coeff = 9.0 / 8.0
outer_coeff = -1.0 / 24.0
advance_time_step = 0.15
axis_of = (1, 2, 0)


def extended(array, sides, width):
    for axis, dim in sides:
        devices, length = (lax.axis_size(axis), array.shape[dim])
        up = [(i, (i + 1) % devices) for i in range(devices - 1)]
        down = [(j, i) for i, j in up]
        last = lax.slice_in_dim(array, length - width, length, axis=dim)
        first = lax.slice_in_dim(array, 0, width, axis=dim)
        before = lax.ppermute(last, axis, up)
        after = lax.ppermute(first, axis, down)
        array = jnp.concatenate([before, array, after], axis=dim)
    return array


def stress_slot(first, second):
    if first == second:
        return first
    return {(0, 1): 3, (1, 0): 3, (0, 2): 4, (2, 0): 4, (1, 2): 5, (2, 1): 5}[first, second]


def window(padded, direction, offset):
    starts = [2, 2, 2]
    starts[direction] = 2 + offset
    limits = [starts[dimension] + padded.shape[dimension] - 4 for dimension in range(3)]
    return lax.slice(padded, starts, limits)


def ahead_diff(padded, direction):
    return inner_coeff * (
        window(padded, direction, 1) - window(padded, direction, 0)
    ) + outer_coeff * (window(padded, direction, 2) - window(padded, direction, -1))


def behind_diff(padded, direction):
    return inner_coeff * (
        window(padded, direction, 0) - window(padded, direction, -1)
    ) + outer_coeff * (window(padded, direction, 1) - window(padded, direction, -2))


def move_velocity(velocity, padded_stress, buoyancy, forcing, step_now):
    result = []
    for first in range(3):
        pieces = []
        for second in range(3):
            component = padded_stress[stress_slot(first, second)]
            if first == second:
                pieces.append(behind_diff(component, axis_of[second]))
            else:
                pieces.append(ahead_diff(component, axis_of[second]))
        updated = velocity[first] + step_now * (buoyancy * (pieces[0] + pieces[1] + pieces[2]))
        if forcing is not None:
            updated = updated + step_now * forcing[first]
        result.append(updated)
    return jnp.stack(result)


def advance_stress(stress, padded_velocity, first_lame_parameter, shear_stiffness, step_now):
    normal_rates = [ahead_diff(padded_velocity[first], axis_of[first]) for first in range(3)]
    dilatation = normal_rates[0] + normal_rates[1] + normal_rates[2]
    updated = [
        stress[first]
        + step_now
        * (first_lame_parameter * dilatation + 2.0 * shear_stiffness * normal_rates[first])
        for first in range(3)
    ]
    shears = []
    for first, second in ((0, 1), (0, 2), (1, 2)):
        shear_rate = behind_diff(padded_velocity[first], axis_of[second]) + behind_diff(
            padded_velocity[second], axis_of[first]
        )
        updated.append(stress[3 + len(shears)] + step_now * shear_stiffness * shear_rate)
        shears.append(shear_rate)
    return (jnp.stack(updated), normal_rates, dilatation, shears)


def imaging_condition(
    forward_pieces_list,
    adjoint_pieces_list,
    forward_velocity_field,
    adjoint_velocity_field,
    adjoint_before,
):
    forward_strain_rates, forward_divergence, forward_shear_terms = forward_pieces_list
    adjoint_strain_rates, adjoint_divergence, adjoint_shear_terms = adjoint_pieces_list
    lambda_sensitivity = forward_divergence * adjoint_divergence
    modulus_term = 2.0 * (
        forward_strain_rates[0] * adjoint_strain_rates[0]
        + forward_strain_rates[1] * adjoint_strain_rates[1]
        + forward_strain_rates[2] * adjoint_strain_rates[2]
    )
    modulus_term = (
        modulus_term
        + forward_shear_terms[0] * adjoint_shear_terms[0]
        + forward_shear_terms[1] * adjoint_shear_terms[1]
        + forward_shear_terms[2] * adjoint_shear_terms[2]
    )
    density_term = (
        forward_velocity_field[0] * (adjoint_velocity_field[0] - adjoint_before[0])
        + forward_velocity_field[1] * (adjoint_velocity_field[1] - adjoint_before[1])
        + forward_velocity_field[2] * (adjoint_velocity_field[2] - adjoint_before[2])
    )
    return jnp.stack([lambda_sensitivity, modulus_term, density_term / advance_time_step])


def pad_depth(values):
    return jnp.pad(values, ((0, 0), (2, 2), (0, 0), (0, 0)))


def shards(
    forward_state,
    adjoint_state,
    first_lame_parameter,
    shear_stiffness,
    buoyancy,
    layer_mask,
    layer_element,
    layer_forces,
):
    forward_wavefield = forward_state[0]
    adjoint_wavefield = adjoint_state[0]
    mask_float = layer_mask.astype(jnp.float32)
    forcing = jnp.stack(
        [mask_float * jnp.take(layer_forces[0, first], layer_element) for first in range(3)]
    )
    both_stresses = extended(
        jnp.concatenate([forward_wavefield[3:], adjoint_wavefield[3:]], 0),
        (("gx", 2), ("gy", 3)),
        2,
    )
    forward_padded = pad_depth(both_stresses[:6])
    adjoint_padded = pad_depth(both_stresses[6:])
    forward_velocity_field = move_velocity(
        forward_wavefield[:3], forward_padded, buoyancy, forcing, advance_time_step
    )
    adjoint_velocity_field = move_velocity(
        adjoint_wavefield[:3], adjoint_padded, buoyancy, None, -advance_time_step
    )
    paired_velocity_fields = pad_depth(
        extended(
            jnp.concatenate([forward_velocity_field, adjoint_velocity_field], 0),
            (("gx", 2), ("gy", 3)),
            2,
        )
    )
    forward_velocity_padded = paired_velocity_fields[:3]
    adjoint_velocity_padded = paired_velocity_fields[3:]
    forward_stress_field, forward_strain_rates, forward_divergence, forward_shear_terms = (
        advance_stress(
            forward_wavefield[3:],
            forward_velocity_padded,
            first_lame_parameter,
            shear_stiffness,
            advance_time_step,
        )
    )
    adjoint_stress_field, adjoint_strain_rates, adjoint_divergence, adjoint_shear_terms = (
        advance_stress(
            adjoint_wavefield[3:],
            adjoint_velocity_padded,
            first_lame_parameter,
            shear_stiffness,
            -advance_time_step,
        )
    )
    sensitivity_terms = imaging_condition(
        (forward_strain_rates, forward_divergence, forward_shear_terms),
        (adjoint_strain_rates, adjoint_divergence, adjoint_shear_terms),
        forward_velocity_field,
        adjoint_velocity_field,
        adjoint_wavefield[:3],
    )
    kernels = lax.psum(sensitivity_terms, "ev")
    forward_next = jnp.concatenate([forward_velocity_field, forward_stress_field], 0)[None]
    return (forward_next, kernels)


def solution(mesh):
    in_specs = (
        P("ev", None, None, "gx", "gy"),
        P("ev", None, None, "gx", "gy"),
        P(None, "gx", "gy"),
        P(None, "gx", "gy"),
        P(None, "gx", "gy"),
        P(None, "gx", "gy"),
        P(None, "gx", "gy"),
        P("ev", None, None),
    )
    out_specs = (P("ev", None, None, "gx", "gy"), P(None, None, "gx", "gy"))
    return jax.shard_map(shards, mesh=mesh, in_specs=in_specs, out_specs=out_specs, check_vma=False)
```

profile of v0, /device:TPU:32, one launch (start us, length us, event | category | flops | bytes accessed | tf_op | source)
XLA Modules:
  0.0 315.8 jit_solution(7231565807432091959)
XLA Ops:
  7.2 1.1 slice_bitcast_fusion.6
  8.3 3.8 %collective-permute-start = (f32[12,4,2,128]{3,2,1,0:T(2,128)S(1)}, f32[12,4,2,128]{3,2,1,0:T(2,128)S(1)}, u32[]{:S(2)}, u32[]{:S(2)}) collective-permute-start(f32[12,4,2,128]{3,2,1,0:T(2,128)S(1)} %get-tuple-element.47), channel_id=1, source_target_pairs={{0,4},{4,8},{8,12},{12,16},{16,20},{20,24},{24,28},{28,32},{32,36}... | collective-permute-start | bytes 147464 | tf_op jit(solution)/shard_map/ppermute | solution.py:19
  12.2 4.8 %collective-permute-start.1 = (f32[12,4,2,128]{3,2,1,0:T(2,128)S(1)}, f32[12,4,2,128]{3,2,1,0:T(2,128)S(1)}, u32[]{:S(2)}, u32[]{:S(2)}) collective-permute-start(f32[12,4,2,128]{3,2,1,0:T(2,128)S(1)} %get-tuple-element.48), channel_id=1, source_target_pairs={{4,0},{8,4},{12,8},{16,12},{20,16},{24,20},{28,24},{32,28},{36,32}... | collective-permute-start | bytes 147464 | tf_op jit(solution)/shard_map/ppermute | solution.py:20
  17.1 1.6 collective-permute-done.1
  19.4 1.3 collective-permute-start.2
  21.1 1.3 collective-permute-start.3
  22.4 51.2 %gather_fusion.1 = f32[8192]{0:T(1024)S(1)} fusion(f32[512]{0:T(512)S(1)} %bitcast.146, s32[8192]{0:T(1024)S(1)} %broadcast_clamp_fusion), kind=kCustom, calls=%fused_computation.1.clone | custom fusion | bytes 98304 | tf_op jit(solution)/shard_map/jit(_take)/gather | solution.py:133
  73.7 51.2 %gather_fusion.2 = f32[8192]{0:T(1024)S(1)} fusion(f32[512]{0:T(512)S(1)} %bitcast.145, s32[8192]{0:T(1024)S(1)} %broadcast_clamp_fusion), kind=kCustom, calls=%fused_computation.2.clone | custom fusion | bytes 98304 | tf_op jit(solution)/shard_map/jit(_take)/gather | solution.py:133
  124.9 51.2 %gather_fusion = f32[8192]{0:T(1024)S(1)} fusion(f32[512]{0:T(512)S(1)} %bitcast.144, s32[8192]{0:T(1024)S(1)} %broadcast_clamp_fusion), kind=kCustom, calls=%fused_computation.clone | custom fusion | bytes 98304 | tf_op jit(solution)/shard_map/jit(_take)/gather | solution.py:133
  176.2 0.4 copy.95
  176.6 0.4 copy.96
  177.0 0.7 pad_maximum_fusion
  178.1 0.8 copy-done.1
  178.9 1.4 fusion.170
  180.4 4.4 %collective-permute-start.4 = (f32[6,4,2,128]{3,2,1,0:T(2,128)S(1)}, f32[6,4,2,128]{3,2,1,0:T(2,128)S(1)}, u32[]{:S(2)}, u32[]{:S(2)}) collective-permute-start(f32[6,4,2,128]{3,2,1,0:T(2,128)S(1)} %get-tuple-element.51), channel_id=1, source_target_pairs={{0,4},{4,8},{8,12},{12,16},{16,20},{20,24},{24,28},{28,32},{32,36}... | collective-permute-start | bytes 73736 | tf_op jit(solution)/shard_map/ppermute | solution.py:19
  184.8 1.9 collective-permute-start.5
  186.7 5.0 %collective-permute-done.5 = f32[6,4,2,128]{3,2,1,0:T(2,128)S(1)} collective-permute-done((f32[6,4,2,128]{3,2,1,0:T(2,128)S(1)}, f32[6,4,2,128]{3,2,1,0:T(2,128)S(1)}, u32[]{:S(2)}, u32[]{:S(2)}) %collective-permute-start.5) | collective-permute-done | bytes 24608 | tf_op jit(solution)/shard_map/ppermute | solution.py:20
  191.9 3.6 %collective-permute-start.6 = (f32[6,4,20,2]{3,2,1,0:T(8,128)S(1)}, f32[6,4,20,2]{3,2,1,0:T(8,128)S(1)}, u32[]{:S(2)}, u32[]{:S(2)}) collective-permute-start(f32[6,4,20,2]{3,2,1,0:T(8,128)S(1)} %get-tuple-element.49), channel_id=1, source_target_pairs={{0,1},{1,2},{2,3},{4,5},{5,6},{6,7},{8,9},{9,10},{10,11},{12,13},{... | collective-permute-start | bytes 11528 | tf_op jit(solution)/shard_map/ppermute | solution.py:19
  195.6 1.3 collective-permute-start.7
  196.9 4.5 %collective-permute-done.7 = f32[6,4,20,2]{3,2,1,0:T(8,128)S(1)} collective-permute-done((f32[6,4,20,2]{3,2,1,0:T(8,128)S(1)}, f32[6,4,20,2]{3,2,1,0:T(8,128)S(1)}, u32[]{:S(2)}, u32[]{:S(2)}) %collective-permute-start.7) | collective-permute-done | bytes 3872 | tf_op jit(solution)/shard_map/ppermute | solution.py:20
  201.4 0.4 select_maximum_fusion
  202.6 0.6 pad_maximum_fusion.3
  203.5 104.0 %all-reduce.5.cloned.1.call-done = f32[3,4,16,128]{3,2,1,0:T(8,128)} async-done(((f32[3,4,16,128]{3,2,1,0:T(8,128)}), f32[3,4,16,128]{3,2,1,0:T(8,128)}) %all-reduce.5.cloned.1.call-update) | async-done | bytes 98320 | tf_op jit(solution)/shard_map/psum | solution.py:182
  307.4 1.5 copy.111
  (51 shorter events, 2.7 us)
Async XLA Ops:
  7.2 9.8 %copy-start.2 = (s32[4,16,128]{2,1,0:T(8,128)S(1)}, s32[4,16,128]{2,1,0:T(8,128)}, u32[]{:S(2)}) copy-start(s32[4,16,128]{2,1,0:T(8,128)} %param.16) | copy-start | bytes 98308
  7.2 300.3 %all-reduce.5.cloned.1.call-start = ((), (), s32[]{:S(2)}) async-start(), calls=%async_computation | async-start | bytes 196608 | tf_op jit(solution)/shard_map/psum | solution.py:182
  8.3 8.8 %collective-permute-start = (f32[12,4,2,128]{3,2,1,0:T(2,128)S(1)}, f32[12,4,2,128]{3,2,1,0:T(2,128)S(1)}, u32[]{:S(2)}, u32[]{:S(2)}) collective-permute-start(f32[12,4,2,128]{3,2,1,0:T(2,128)S(1)} %get-tuple-element.47), channel_id=1, source_target_pairs={{0,4},{4,8},{8,12},{12,16},{16,20},{20,24},{24,28},{28,32},{32,36}... | collective-permute-start | bytes 147464 | tf_op jit(solution)/shard_map/ppermute | solution.py:19
  12.2 6.6 %collective-permute-start.1 = (f32[12,4,2,128]{3,2,1,0:T(2,128)S(1)}, f32[12,4,2,128]{3,2,1,0:T(2,128)S(1)}, u32[]{:S(2)}, u32[]{:S(2)}) collective-permute-start(f32[12,4,2,128]{3,2,1,0:T(2,128)S(1)} %get-tuple-element.48), channel_id=1, source_target_pairs={{4,0},{8,4},{12,8},{16,12},{20,16},{24,20},{28,24},{32,28},{36,32}... | collective-permute-start | bytes 147464 | tf_op jit(solution)/shard_map/ppermute | solution.py:20
  19.0 3.4 %copy-start.6 = (f32[1,3,512]{2,0,1:T(1,128)S(1)}, f32[1,3,512]{2,0,1:T(1,128)}, u32[]{:S(2)}) copy-start(f32[1,3,512]{2,0,1:T(1,128)} %param.17) | copy-start | bytes 18436
  19.4 156.7 %collective-permute-start.2 = (f32[12,4,20,2]{2,1,3,0:T(4,128)S(1)}, f32[12,4,20,2]{2,1,3,0:T(4,128)S(1)}, u32[]{:S(2)}, u32[]{:S(2)}) collective-permute-start(f32[12,4,20,2]{2,1,3,0:T(4,128)S(1)} %copy.93), channel_id=1, source_target_pairs={{0,1},{1,2},{2,3},{4,5},{5,6},{6,7},{8,9},{9,10},{10,11},{12,13},{... | collective-permute-start | bytes 23048 | tf_op jit(solution)/shard_map/ppermute | solution.py:19
  21.1 155.4 %collective-permute-start.3 = (f32[12,4,20,2]{2,1,3,0:T(4,128)S(1)}, f32[12,4,20,2]{2,1,3,0:T(4,128)S(1)}, u32[]{:S(2)}, u32[]{:S(2)}) collective-permute-start(f32[12,4,20,2]{2,1,3,0:T(4,128)S(1)} %copy.94), channel_id=1, source_target_pairs={{1,0},{2,1},{3,2},{5,4},{6,5},{7,6},{9,8},{10,9},{11,10},{13,12},{... | collective-permute-start | bytes 23048 | tf_op jit(solution)/shard_map/ppermute | solution.py:20
  177.9 1.0 copy-start.1
  178.0 1.0 copy-start.3
  178.0 0.9 copy-start.4
  180.4 6.3 %collective-permute-start.4 = (f32[6,4,2,128]{3,2,1,0:T(2,128)S(1)}, f32[6,4,2,128]{3,2,1,0:T(2,128)S(1)}, u32[]{:S(2)}, u32[]{:S(2)}) collective-permute-start(f32[6,4,2,128]{3,2,1,0:T(2,128)S(1)} %get-tuple-element.51), channel_id=1, source_target_pairs={{0,4},{4,8},{8,12},{12,16},{16,20},{20,24},{24,28},{28,32},{32,36}... | collective-permute-start | bytes 73736 | tf_op jit(solution)/shard_map/ppermute | solution.py:19
  184.8 6.9 %collective-permute-start.5 = (f32[6,4,2,128]{3,2,1,0:T(2,128)S(1)}, f32[6,4,2,128]{3,2,1,0:T(2,128)S(1)}, u32[]{:S(2)}, u32[]{:S(2)}) collective-permute-start(f32[6,4,2,128]{3,2,1,0:T(2,128)S(1)} %get-tuple-element.52), channel_id=1, source_target_pairs={{4,0},{8,4},{12,8},{16,12},{20,16},{24,20},{28,24},{32,28},{36,32}... | collective-permute-start | bytes 73736 | tf_op jit(solution)/shard_map/ppermute | solution.py:20
  191.9 4.9 %collective-permute-start.6 = (f32[6,4,20,2]{3,2,1,0:T(8,128)S(1)}, f32[6,4,20,2]{3,2,1,0:T(8,128)S(1)}, u32[]{:S(2)}, u32[]{:S(2)}) collective-permute-start(f32[6,4,20,2]{3,2,1,0:T(8,128)S(1)} %get-tuple-element.49), channel_id=1, source_target_pairs={{0,1},{1,2},{2,3},{4,5},{5,6},{6,7},{8,9},{9,10},{10,11},{12,13},{... | collective-permute-start | bytes 11528 | tf_op jit(solution)/shard_map/ppermute | solution.py:19
  195.6 5.8 %collective-permute-start.7 = (f32[6,4,20,2]{3,2,1,0:T(8,128)S(1)}, f32[6,4,20,2]{3,2,1,0:T(8,128)S(1)}, u32[]{:S(2)}, u32[]{:S(2)}) collective-permute-start(f32[6,4,20,2]{3,2,1,0:T(8,128)S(1)} %get-tuple-element.50), channel_id=1, source_target_pairs={{1,0},{2,1},{3,2},{5,4},{6,5},{7,6},{9,8},{10,9},{11,10},{13,12},{... | collective-permute-start | bytes 11528 | tf_op jit(solution)/shard_map/ppermute | solution.py:20
  202.2 1.1 copy-start
  202.2 1.1 copy-start.5
  203.5 105.5 %copy-start.7 = (f32[9,4,16,128]{3,2,1,0:T(8,128)}, f32[9,4,16,128]{3,2,1,0:T(8,128)S(1)}, u32[]{:S(2)}) copy-start(f32[9,4,16,128]{3,2,1,0:T(8,128)S(1)} %bitcast_dynamic-update-slice_fusion) | copy-start | bytes 884740
Sparse Core Ops, SparseCore 0:
  203.4 103.9 all-reduce.4
where the time goes:
time: 316 us
  local copies, waits for them, and re-layouts  160 us (51%)
  waiting for transfers between devices  115 us (36%)
  starting transfers between devices  22.5 us (7%)
  between operations  14.4 us (5%)
  other arithmetic  4.16 us (1%)
    gather x3, local copies, waits for them, and re-layouts, shards(): jnp.take(layer_forces[0, first], layer_element)  154 us
    psum x1, waiting for transfers between devices, shards(): kernels = lax.psum(sensitivity_terms, 'ev')  104 us
    ppermute x4, starting transfers between devices, extended(): before = lax.ppermute(last, axis, up)  13.1 us
    ppermute x4, waiting for transfers between devices, extended(): after = lax.ppermute(first, axis, down)  11.1 us
    ppermute x4, starting transfers between devices, extended(): after = lax.ppermute(first, axis, down)  9.32 us
  transfers between devices with their start and end apart: 9, of which 5 were waited for; matrix products, arithmetic and copies ran while one was open for 49% of the time, Pallas kernels for 0%

commit v1 on v0

--- a/solution.py
+++ b/solution.py
@@ -1,6 +1,8 @@
 import jax
 import jax.numpy as jnp
 from jax import lax
+from jax.experimental import pallas as pl
+from jax.experimental.pallas import tpu as pltpu
 from jax.sharding import PartitionSpec as P
 
 inner_coeff = 9.0 / 8.0
@@ -112,6 +114,41 @@
     return jnp.stack([lambda_sensitivity, modulus_term, density_term / advance_time_step])
 
 
+def lookup(mask_ref, element_ref, table_ref, out_ref):
+    depth, rows, lanes = element_ref.shape
+    for z in range(depth):
+        for row in range(0, rows, 8):
+            element = element_ref[z, row : row + 8, :]
+            weight = mask_ref[z, row : row + 8, :].astype(jnp.float32)
+            lane = jnp.bitwise_and(element, 127)
+            part = jnp.right_shift(element, 7)
+            for first in range(3):
+                found = jnp.zeros((8, lanes), jnp.float32)
+                for k in range(table_ref.shape[1]):
+                    entries = jnp.broadcast_to(table_ref[first, k : k + 1, :], (8, lanes))
+                    taken = jnp.take_along_axis(entries, lane, axis=1, mode="promise_in_bounds")
+                    found = jnp.where(part == k, taken, found)
+                out_ref[first, z, row : row + 8, :] = weight * found
+
+
+def force_field(layer_mask, layer_element, layer_forces):
+    table = layer_forces.reshape(3, -1, 128)
+    return pl.pallas_call(
+        lookup,
+        out_shape=jax.ShapeDtypeStruct((3,) + layer_mask.shape, jnp.float32),
+        in_specs=[pl.BlockSpec(memory_space=pltpu.VMEM)] * 3,
+        out_specs=pl.BlockSpec(memory_space=pltpu.VMEM),
+    )(layer_mask, layer_element, table)
+
+
+def event_sum(terms):
+    events = lax.axis_size("ev")
+    flat = terms.reshape(-1, 8, 128)
+    sent = jnp.broadcast_to(flat[None], (events,) + flat.shape)
+    got = lax.all_to_all(sent, "ev", 0, 0, tiled=True)
+    return jnp.sum(got, axis=0).reshape(terms.shape)
+
+
 def pad_depth(values):
     return jnp.pad(values, ((0, 0), (2, 2), (0, 0), (0, 0)))
 
@@ -128,10 +165,7 @@
 ):
     forward_wavefield = forward_state[0]
     adjoint_wavefield = adjoint_state[0]
-    mask_float = layer_mask.astype(jnp.float32)
-    forcing = jnp.stack(
-        [mask_float * jnp.take(layer_forces[0, first], layer_element) for first in range(3)]
-    )
+    forcing = force_field(layer_mask, layer_element, layer_forces)
     both_stresses = extended(
         jnp.concatenate([forward_wavefield[3:], adjoint_wavefield[3:]], 0),
         (("gx", 2), ("gy", 3)),
@@ -179,7 +213,7 @@
         adjoint_velocity_field,
         adjoint_wavefield[:3],
     )
-    kernels = lax.psum(sensitivity_terms, "ev")
+    kernels = event_sum(sensitivity_terms)
     forward_next = jnp.concatenate([forward_velocity_field, forward_stress_field], 0)[None]
     return (forward_next, kernels)
 

time: 316 us -> 68.6 us (0.22)
  the two profiles are of different devices: /device:TPU:32 before, /device:TPU:193 now
where the time goes in v1:
time: 68.6 us; the launch traced here: 68.1 us
  starting transfers between devices  30.9 us (45%)
  waiting for transfers between devices  25.2 us (37%)
  local copies, waits for them, and re-layouts  5.26 us (8%)
  other arithmetic  4.17 us (6%)
  Pallas kernels  1.63 us (2%)
  between operations  0.97 us (1%)
    ppermute x4, starting transfers between devices, extended(): before = lax.ppermute(last, axis, up)  16.9 us
    ppermute x4, waiting for transfers between devices, extended(): after = lax.ppermute(first, axis, down)  12.8 us
    all_to_all x1, waiting for transfers between devices, event_sum(): got = lax.all_to_all(sent, 'ev', 0, 0, tiled=True)  10.7 us
    ppermute x4, starting transfers between devices, extended(): after = lax.ppermute(first, axis, down)  7.67 us
    all_to_all x1, starting transfers between devices, event_sum(): got = lax.all_to_all(sent, 'ev', 0, 0, tiled=True)  6.36 us
    another operation x4, other arithmetic, imaging_condition(): jnp.stack([lambda_sensitivity, modulus_term, density_term / advance_time_...  2.1 us
    ppermute x4, waiting for transfers between devices, extended(): before = lax.ppermute(last, axis, up)  1.73 us
    pallas_call x1, Pallas kernels, force_field(): pl.pallas_call(lookup, out_shape=jax.ShapeDtypeStruct((3,) + layer_mask.s...  1.63 us
  transfers between devices with their start and end apart: 9, of which 6 were waited for; matrix products, arithmetic and copies ran while one was open for 1% of the time, Pallas kernels for 2%

profile of v1, /device:TPU:193, one launch (start us, length us, event | category | flops | bytes accessed | tf_op | source)
XLA Modules:
  0.0 68.1 jit_solution(8891729280862580233)
XLA Ops:
  0.6 1.1 %slice_bitcast_fusion.6 = (f32[6,4,16,128]{3,2,1,0:T(8,128)S(1)}, f32[6,4,16,128]{3,2,1,0:T(8,128)S(1)}) fusion(f32[1,9,4,16,128]{4,3,2,1,0:T(8,128)} %param.9, f32[1,9,4,16,128]{4,3,2,1,0:T(8,128)} %param.8), kind=kLoop, calls=%fused_computation.40 | loop fusion | bytes 786432 | tf_op jit(solution)/shard_map/slice | solution.py:170
  1.7 3.5 %collective-permute-start = (f32[12,4,2,128]{3,2,1,0:T(2,128)S(1)}, f32[12,4,2,128]{3,2,1,0:T(2,128)S(1)}, u32[]{:S(2)}, u32[]{:S(2)}) collective-permute-start(f32[12,4,2,128]{3,2,1,0:T(2,128)S(1)} %get-tuple-element.44), channel_id=1, source_target_pairs={{0,4},{4,8},{8,12},{12,16},{16,20},{20,24},{24,28},{28,32},{32,36}... | collective-permute-start | bytes 147464 | tf_op jit(solution)/shard_map/ppermute | solution.py:21
  5.3 1.9 %collective-permute-start.1 = (f32[12,4,2,128]{3,2,1,0:T(2,128)S(1)}, f32[12,4,2,128]{3,2,1,0:T(2,128)S(1)}, u32[]{:S(2)}, u32[]{:S(2)}) collective-permute-start(f32[12,4,2,128]{3,2,1,0:T(2,128)S(1)} %get-tuple-element.45), channel_id=1, source_target_pairs={{4,0},{8,4},{12,8},{16,12},{20,16},{24,20},{28,24},{32,28},{36,32}... | collective-permute-start | bytes 147464 | tf_op jit(solution)/shard_map/ppermute | solution.py:22
  7.2 4.3 %collective-permute-done.1 = f32[12,4,2,128]{3,2,1,0:T(2,128)S(1)} collective-permute-done((f32[12,4,2,128]{3,2,1,0:T(2,128)S(1)}, f32[12,4,2,128]{3,2,1,0:T(2,128)S(1)}, u32[]{:S(2)}, u32[]{:S(2)}) %collective-permute-start.1) | collective-permute-done | bytes 49184 | tf_op jit(solution)/shard_map/ppermute | solution.py:22
  12.2 4.8 %collective-permute-start.2 = (f32[12,4,20,2]{2,1,3,0:T(4,128)S(1)}, f32[12,4,20,2]{2,1,3,0:T(4,128)S(1)}, u32[]{:S(2)}, u32[]{:S(2)}) collective-permute-start(f32[12,4,20,2]{2,1,3,0:T(4,128)S(1)} %copy.14), channel_id=1, source_target_pairs={{0,1},{1,2},{2,3},{4,5},{5,6},{6,7},{8,9},{9,10},{10,11},{12,13},{... | collective-permute-start | bytes 23048 | tf_op jit(solution)/shard_map/ppermute | solution.py:21
  17.4 1.9 %collective-permute-start.3 = (f32[12,4,20,2]{2,1,3,0:T(4,128)S(1)}, f32[12,4,20,2]{2,1,3,0:T(4,128)S(1)}, u32[]{:S(2)}, u32[]{:S(2)}) collective-permute-start(f32[12,4,20,2]{2,1,3,0:T(4,128)S(1)} %copy.15), channel_id=1, source_target_pairs={{1,0},{2,1},{3,2},{5,4},{6,5},{7,6},{9,8},{10,9},{11,10},{13,12},{... | collective-permute-start | bytes 23048 | tf_op jit(solution)/shard_map/ppermute | solution.py:22
  19.4 1.6 %shard_map.95 = f32[3,4,16,128]{3,2,1,0:T(8,128)} custom-call(s32[4,16,128]{2,1,0:T(8,128)} %mask_ref.1, s32[4,16,128]{2,1,0:T(8,128)} %element_ref.1, f32[3,4,128]{2,1,0:T(4,128)} %bitcast.157), custom_call_target="tpu_custom_call" | custom-call | tf_op jit(solution)/shard_map/pallas_call | solution.py:136
  21.0 0.4 copy.16
  21.4 1.4 %collective-permute-done.3 = f32[12,4,20,2]{2,1,3,0:T(4,128)S(1)} collective-permute-done((f32[12,4,20,2]{2,1,3,0:T(4,128)S(1)}, f32[12,4,20,2]{2,1,3,0:T(4,128)S(1)}, u32[]{:S(2)}, u32[]{:S(2)}) %collective-permute-start.3) | collective-permute-done | bytes 7712 | tf_op jit(solution)/shard_map/ppermute | solution.py:22
  22.8 0.4 copy.17
  23.3 0.7 %pad_maximum_fusion = f32[12,4,20,132]{3,2,1,0:T(8,128)S(1)} fusion(f32[12,4,20,2]{3,2,1,0:T(8,128)S(1)} %copy.17, f32[12,4,2,128]{3,2,1,0:T(2,128)S(1)} %collective-permute-done.1, f32[6,4,16,128]{3,2,1,0:T(8,128)S(1)} %get-tuple-element.56, f32[6,4,16,128]{3,2,1,0:T(8,128)S(1)} %get-tuple-element.57, f32[12,4,2,128]{3,2,1,0:T(2,128)S(1)} %collective-permute-done, ...), kind=kLoop, calls=%fused_computation.18 | loop fusion | flops 633600 | bytes 1013760 | tf_op jit(solution)/shard_map/concatenate | solution.py:23
  24.3 0.8 %copy-done.1 = f32[1,9,4,16,128]{4,3,2,1,0:T(8,128)S(1)} copy-done((f32[1,9,4,16,128]{4,3,2,1,0:T(8,128)S(1)}, f32[1,9,4,16,128]{4,3,2,1,0:T(8,128)}, u32[]{:S(2)}) %copy-start.1) | copy-done | bytes 294936
  25.2 1.4 %fusion.173 = (f32[1,4,16,128]{3,2,1,0:T(8,128)S(1)}, f32[4,16,128]{2,1,0:T(8,128)S(1)}, f32[4,16,128]{2,1,0:T(8,128)S(1)}, f32[4,16,128]{2,1,0:T(8,128)S(1)}, f...) fusion(f32[1,9,4,16,128]{4,3,2,1,0:T(8,128)} %param.9, ...), kind=kLoop, calls=%fused_computation.301 | loop fusion | flops 1105920 | bytes 2719744 | tf_op jit(solution)/shard_map/stack | solution.py:114
  26.7 4.9 %collective-permute-start.4 = (f32[6,4,2,128]{3,2,1,0:T(2,128)S(1)}, f32[6,4,2,128]{3,2,1,0:T(2,128)S(1)}, u32[]{:S(2)}, u32[]{:S(2)}) collective-permute-start(f32[6,4,2,128]{3,2,1,0:T(2,128)S(1)} %get-tuple-element.48), channel_id=1, source_target_pairs={{0,4},{4,8},{8,12},{12,16},{16,20},{20,24},{24,28},{28,32},{32,36}... | collective-permute-start | bytes 73736 | tf_op jit(solution)/shard_map/ppermute | solution.py:21
  31.6 1.9 %collective-permute-start.5 = (f32[6,4,2,128]{3,2,1,0:T(2,128)S(1)}, f32[6,4,2,128]{3,2,1,0:T(2,128)S(1)}, u32[]{:S(2)}, u32[]{:S(2)}) collective-permute-start(f32[6,4,2,128]{3,2,1,0:T(2,128)S(1)} %get-tuple-element.49), channel_id=1, source_target_pairs={{4,0},{8,4},{12,8},{16,12},{20,16},{24,20},{28,24},{32,28},{36,32}... | collective-permute-start | bytes 73736 | tf_op jit(solution)/shard_map/ppermute | solution.py:22
  33.5 2.6 %collective-permute-done.5 = f32[6,4,2,128]{3,2,1,0:T(2,128)S(1)} collective-permute-done((f32[6,4,2,128]{3,2,1,0:T(2,128)S(1)}, f32[6,4,2,128]{3,2,1,0:T(2,128)S(1)}, u32[]{:S(2)}, u32[]{:S(2)}) %collective-permute-start.5) | collective-permute-done | bytes 24608 | tf_op jit(solution)/shard_map/ppermute | solution.py:22
  36.3 3.6 %collective-permute-start.6 = (f32[6,4,20,2]{3,2,1,0:T(8,128)S(1)}, f32[6,4,20,2]{3,2,1,0:T(8,128)S(1)}, u32[]{:S(2)}, u32[]{:S(2)}) collective-permute-start(f32[6,4,20,2]{3,2,1,0:T(8,128)S(1)} %get-tuple-element.46), channel_id=1, source_target_pairs={{0,1},{1,2},{2,3},{4,5},{5,6},{6,7},{8,9},{9,10},{10,11},{12,13},{... | collective-permute-start | bytes 11528 | tf_op jit(solution)/shard_map/ppermute | solution.py:21
  40.0 1.9 %collective-permute-start.7 = (f32[6,4,20,2]{3,2,1,0:T(8,128)S(1)}, f32[6,4,20,2]{3,2,1,0:T(8,128)S(1)}, u32[]{:S(2)}, u32[]{:S(2)}) collective-permute-start(f32[6,4,20,2]{3,2,1,0:T(8,128)S(1)} %get-tuple-element.47), channel_id=1, source_target_pairs={{1,0},{2,1},{3,2},{5,4},{6,5},{7,6},{9,8},{10,9},{11,10},{13,12},{... | collective-permute-start | bytes 11528 | tf_op jit(solution)/shard_map/ppermute | solution.py:22
  41.9 1.7 %collective-permute-done.6 = f32[6,4,20,2]{3,2,1,0:T(8,128)S(1)} collective-permute-done((f32[6,4,20,2]{3,2,1,0:T(8,128)S(1)}, f32[6,4,20,2]{3,2,1,0:T(8,128)S(1)}, u32[]{:S(2)}, u32[]{:S(2)}) %collective-permute-start.6) | collective-permute-done | bytes 3872 | tf_op jit(solution)/shard_map/ppermute | solution.py:21
  43.6 4.4 %collective-permute-done.7 = f32[6,4,20,2]{3,2,1,0:T(8,128)S(1)} collective-permute-done((f32[6,4,20,2]{3,2,1,0:T(8,128)S(1)}, f32[6,4,20,2]{3,2,1,0:T(8,128)S(1)}, u32[]{:S(2)}, u32[]{:S(2)}) %collective-permute-start.7) | collective-permute-done | bytes 3872 | tf_op jit(solution)/shard_map/ppermute | solution.py:22
  49.3 0.9 %broadcast_in_dim.12 = f32[8,24,8,128]{3,2,1,0:T(8,128)} broadcast(f32[24,8,128]{2,1,0:T(8,128)S(1)} %bitcast.155), dimensions={1,2,3} | broadcast | bytes 884736 | tf_op jit(solution)/shard_map/broadcast_in_dim | solution.py:147
  50.2 6.4 %all-to-all-start = ((f32[8,24,8,128]{3,2,1,0:T(8,128)}), f32[8,24,8,128]{3,2,1,0:T(8,128)S(1)}, u32[]{:S(2)}, u32[]{:S(2)}) async-start(f32[8,24,8,128]{3,2,1,0:T(8,128)} %broadcast_in_dim.12), calls=%async_computation | async-start | bytes 1572864 | tf_op jit(solution)/shard_map/all_to_all | solution.py:148
  56.7 10.7 %all-to-all-done = f32[8,24,8,128]{3,2,1,0:T(8,128)S(1)} async-done(((f32[8,24,8,128]{3,2,1,0:T(8,128)}), f32[8,24,8,128]{3,2,1,0:T(8,128)S(1)}, u32[]{:S(2)}, u32[]{:S(2)}) %all-to-all-start) | async-done | bytes 786464 | tf_op jit(solution)/shard_map/all_to_all | solution.py:148
  67.4 0.7 reduce_sum.9
  (42 shorter events, 3.0 us)
Async XLA Ops:
  1.7 5.5 %collective-permute-start = (f32[12,4,2,128]{3,2,1,0:T(2,128)S(1)}, f32[12,4,2,128]{3,2,1,0:T(2,128)S(1)}, u32[]{:S(2)}, u32[]{:S(2)}) collective-permute-start(f32[12,4,2,128]{3,2,1,0:T(2,128)S(1)} %get-tuple-element.44), channel_id=1, source_target_pairs={{0,4},{4,8},{8,12},{12,16},{16,20},{20,24},{24,28},{28,32},{32,36}... | collective-permute-start | bytes 147464 | tf_op jit(solution)/shard_map/ppermute | solution.py:21
  5.3 6.2 %collective-permute-start.1 = (f32[12,4,2,128]{3,2,1,0:T(2,128)S(1)}, f32[12,4,2,128]{3,2,1,0:T(2,128)S(1)}, u32[]{:S(2)}, u32[]{:S(2)}) collective-permute-start(f32[12,4,2,128]{3,2,1,0:T(2,128)S(1)} %get-tuple-element.45), channel_id=1, source_target_pairs={{4,0},{8,4},{12,8},{16,12},{20,16},{24,20},{28,24},{32,28},{36,32}... | collective-permute-start | bytes 147464 | tf_op jit(solution)/shard_map/ppermute | solution.py:22
  12.2 8.8 %collective-permute-start.2 = (f32[12,4,20,2]{2,1,3,0:T(4,128)S(1)}, f32[12,4,20,2]{2,1,3,0:T(4,128)S(1)}, u32[]{:S(2)}, u32[]{:S(2)}) collective-permute-start(f32[12,4,20,2]{2,1,3,0:T(4,128)S(1)} %copy.14), channel_id=1, source_target_pairs={{0,1},{1,2},{2,3},{4,5},{5,6},{6,7},{8,9},{9,10},{10,11},{12,13},{... | collective-permute-start | bytes 23048 | tf_op jit(solution)/shard_map/ppermute | solution.py:21
  17.4 5.4 %collective-permute-start.3 = (f32[12,4,20,2]{2,1,3,0:T(4,128)S(1)}, f32[12,4,20,2]{2,1,3,0:T(4,128)S(1)}, u32[]{:S(2)}, u32[]{:S(2)}) collective-permute-start(f32[12,4,20,2]{2,1,3,0:T(4,128)S(1)} %copy.15), channel_id=1, source_target_pairs={{1,0},{2,1},{3,2},{5,4},{6,5},{7,6},{9,8},{10,9},{11,10},{13,12},{... | collective-permute-start | bytes 23048 | tf_op jit(solution)/shard_map/ppermute | solution.py:22
  24.2 1.0 %copy-start.1 = (f32[1,9,4,16,128]{4,3,2,1,0:T(8,128)S(1)}, f32[1,9,4,16,128]{4,3,2,1,0:T(8,128)}, u32[]{:S(2)}) copy-start(f32[1,9,4,16,128]{4,3,2,1,0:T(8,128)} %param.8) | copy-start | bytes 884740
  24.2 1.0 %copy-start.2 = (f32[3,4,16,128]{3,2,1,0:T(8,128)S(1)}, f32[3,4,16,128]{3,2,1,0:T(8,128)}, u32[]{:S(2)}) copy-start(f32[3,4,16,128]{3,2,1,0:T(8,128)} %shard_map.95) | copy-start | bytes 294916
  24.2 1.0 %copy-start.3 = (f32[4,16,128]{2,1,0:T(8,128)S(1)}, f32[4,16,128]{2,1,0:T(8,128)}, u32[]{:S(2)}) copy-start(f32[4,16,128]{2,1,0:T(8,128)} %param.12) | copy-start | bytes 98308
  26.7 6.8 %collective-permute-start.4 = (f32[6,4,2,128]{3,2,1,0:T(2,128)S(1)}, f32[6,4,2,128]{3,2,1,0:T(2,128)S(1)}, u32[]{:S(2)}, u32[]{:S(2)}) collective-permute-start(f32[6,4,2,128]{3,2,1,0:T(2,128)S(1)} %get-tuple-element.48), channel_id=1, source_target_pairs={{0,4},{4,8},{8,12},{12,16},{16,20},{20,24},{24,28},{28,32},{32,36}... | collective-permute-start | bytes 73736 | tf_op jit(solution)/shard_map/ppermute | solution.py:21
  31.6 4.6 %collective-permute-start.5 = (f32[6,4,2,128]{3,2,1,0:T(2,128)S(1)}, f32[6,4,2,128]{3,2,1,0:T(2,128)S(1)}, u32[]{:S(2)}, u32[]{:S(2)}) collective-permute-start(f32[6,4,2,128]{3,2,1,0:T(2,128)S(1)} %get-tuple-element.49), channel_id=1, source_target_pairs={{4,0},{8,4},{12,8},{16,12},{20,16},{24,20},{28,24},{32,28},{36,32}... | collective-permute-start | bytes 73736 | tf_op jit(solution)/shard_map/ppermute | solution.py:22
  36.3 7.3 %collective-permute-start.6 = (f32[6,4,20,2]{3,2,1,0:T(8,128)S(1)}, f32[6,4,20,2]{3,2,1,0:T(8,128)S(1)}, u32[]{:S(2)}, u32[]{:S(2)}) collective-permute-start(f32[6,4,20,2]{3,2,1,0:T(8,128)S(1)} %get-tuple-element.46), channel_id=1, source_target_pairs={{0,1},{1,2},{2,3},{4,5},{5,6},{6,7},{8,9},{9,10},{10,11},{12,13},{... | collective-permute-start | bytes 11528 | tf_op jit(solution)/shard_map/ppermute | solution.py:21
  40.0 8.0 %collective-permute-start.7 = (f32[6,4,20,2]{3,2,1,0:T(8,128)S(1)}, f32[6,4,20,2]{3,2,1,0:T(8,128)S(1)}, u32[]{:S(2)}, u32[]{:S(2)}) collective-permute-start(f32[6,4,20,2]{3,2,1,0:T(8,128)S(1)} %get-tuple-element.47), channel_id=1, source_target_pairs={{1,0},{2,1},{3,2},{5,4},{6,5},{7,6},{9,8},{10,9},{11,10},{13,12},{... | collective-permute-start | bytes 11528 | tf_op jit(solution)/shard_map/ppermute | solution.py:22
  49.2 7.3 %copy-start = (f32[4,16,128]{2,1,0:T(8,128)S(1)}, f32[4,16,128]{2,1,0:T(8,128)}, u32[]{:S(2)}) copy-start(f32[4,16,128]{2,1,0:T(8,128)} %param.11) | copy-start | bytes 98308
  49.2 7.3 %copy-start.4 = (f32[4,16,128]{2,1,0:T(8,128)S(1)}, f32[4,16,128]{2,1,0:T(8,128)}, u32[]{:S(2)}) copy-start(f32[4,16,128]{2,1,0:T(8,128)} %param.10) | copy-start | bytes 98308
  50.2 17.2 %all-to-all-start = ((f32[8,24,8,128]{3,2,1,0:T(8,128)}), f32[8,24,8,128]{3,2,1,0:T(8,128)S(1)}, u32[]{:S(2)}, u32[]{:S(2)}) async-start(f32[8,24,8,128]{3,2,1,0:T(8,128)} %broadcast_in_dim.12), calls=%async_computation | async-start | bytes 1572864 | tf_op jit(solution)/shard_map/all_to_all | solution.py:148
  56.7 11.4 %copy-start.5 = (f32[9,4,16,128]{3,2,1,0:T(8,128)}, f32[9,4,16,128]{3,2,1,0:T(8,128)S(1)}, u32[]{:S(2)}) copy-start(f32[9,4,16,128]{3,2,1,0:T(8,128)S(1)} %constant_dynamic-update-slice_fusion.6) | copy-start | bytes 884740

commit v2 on v0

v2 whole, which is shorter than its diff:
```python
import functools

import jax
import jax.numpy as jnp
from jax import lax
from jax.experimental import pallas as pl
from jax.experimental.pallas import tpu as pltpu
from jax.sharding import PartitionSpec as P

inner_coeff = 9.0 / 8.0
outer_coeff = -1.0 / 24.0
advance_time_step = 0.15
vmem_limit = 16 << 20

VX, VY, VZ, SXX, SYY, SZZ, SXY, SXZ, SYZ = range(9)
ADJOINT = 9
BUOYANCY = 18
FIELDS = 19
SUB, LANE = 8, 128
RING = 24
SLOT = 6
SLOTS = 21


def row_slots(depth):
    three = [
        (base + field, z)
        for z in range(depth)
        for base in (0, ADJOINT)
        for field in (SXX, SXY, SXZ)
    ]
    two = [
        (field, z)
        for z in range(depth)
        for field in range(FIELDS)
        if field == BUOYANCY or field % ADJOINT not in (SXX, SXY, SXZ)
    ]
    slots, tile, sub = [], 0, 0
    while three or two:
        if three and sub <= 3:
            (field, z), rows = three.pop(0), 3
        else:
            (field, z), rows = two.pop(0), 2
        slots.append((field, z, rows, tile, sub))
        sub += rows
        if sub + 2 > SUB:
            tile, sub = tile + 1, 0
    return slots, tile + (sub > 0)


def column_slots(depth):
    return [(field, z) for z in range(depth) for field in range(FIELDS)]


def turn(value, amount, axis):
    amount %= value.shape[axis]
    return pltpu.roll(value, amount, axis) if amount else value


def sublanes():
    return lax.broadcasted_iota(jnp.int32, (SUB, LANE), 0)


def column_slot_of():
    return jnp.bitwise_and(lax.broadcasted_iota(jnp.int32, (SUB, LANE), 1) + 3, LANE - 1)


def even(axis):
    return jnp.bitwise_and(lax.axis_index(axis), 1) == 0


def pick(condition, first, second):
    return jnp.where(jnp.broadcast_to(condition, first.shape), first, second)


def lookup(mask_ref, element_ref, table_ref, z, row):
    element = element_ref[z, row : row + SUB, :]
    weight = mask_ref[z, row : row + SUB, :].astype(jnp.float32)
    lane = jnp.bitwise_and(element, LANE - 1)
    part = jnp.right_shift(element, 7)
    parts = table_ref.shape[2] // LANE
    found = []
    for first in range(3):
        value = None
        for k in range(parts):
            part_lanes = slice(LANE * k, LANE * (k + 1))
            entries = jnp.broadcast_to(table_ref[first, :, part_lanes], (SUB, LANE))
            taken = jnp.take_along_axis(entries, lane, axis=1, mode="promise_in_bounds")
            value = taken if k == 0 else jnp.where(part == k, taken, value)
        found.append(weight * value)
    return found


def pack_columns(load, depth, write):
    slot = column_slot_of()
    value = None
    slots = column_slots(depth)
    for k, (field, z) in enumerate(slots):
        tile, place = divmod(k, SLOTS)
        moved = turn(load(field, z), SLOT * place, 1)
        if place == 0:
            value = moved
        else:
            value = jnp.where(slot >= SLOT * place, moved, value)
        if place == SLOTS - 1 or k == len(slots) - 1:
            write(tile, value)


def first_pack(
    forward_hbm,
    adjoint_hbm,
    buoyancy_hbm,
    mask_hbm,
    element_hbm,
    table_hbm,
    first_ref,
    second_ref,
    columns_ref,
    pushed_ref,
    forward_ref,
    adjoint_ref,
    buoyancy_ref,
    mask_ref,
    element_ref,
    table_ref,
    arrivals,
):
    depth, rows, _ = buoyancy_ref.shape
    loads = [
        pltpu.make_async_copy(source, target, arrivals.at[k])
        for k, (source, target) in enumerate(
            (
                (element_hbm, element_ref),
                (mask_hbm, mask_ref),
                (table_hbm, table_ref),
                (forward_hbm, forward_ref),
                (buoyancy_hbm, buoyancy_ref),
                (adjoint_hbm, adjoint_ref),
            )
        )
    ]
    for copy in loads:
        copy.start()
    for copy in loads[:4]:
        copy.wait()
    for z in range(depth):
        for row in range(0, rows, SUB):
            forcing = lookup(mask_ref, element_ref, table_ref, z, row)
            for i in range(3):
                velocity = forward_ref[0, i, z, row : row + SUB, :]
                pushed_ref[i, z, row : row + SUB, :] = velocity + advance_time_step * forcing[i]
    for copy in loads[4:]:
        copy.wait()

    def load(field, z, row):
        if field == BUOYANCY:
            return buoyancy_ref[z, row : row + SUB, :]
        if field >= ADJOINT:
            return adjoint_ref[0, field - ADJOINT, z, row : row + SUB, :]
        if field < 3:
            return pushed_ref[field, z, row : row + SUB, :]
        return forward_ref[0, field, z, row : row + SUB, :]

    slots, tiles = row_slots(depth)
    sub = sublanes()
    is_even = even("gx")
    for tile in range(tiles):
        up, down = None, None
        for field, z, count, at, start in slots:
            if at != tile:
                continue
            last = turn(load(field, z, rows - SUB), start + count, 0)
            first = turn(load(field, z, 0), start, 0)
            up = last if up is None else jnp.where(sub >= start, last, up)
            down = first if down is None else jnp.where(sub >= start, first, down)
        first_ref[tile] = pick(is_even, up, down)
        second_ref[tile] = pick(is_even, down, up)

    for row in range(0, rows, SUB):

        def write(tile, value, row=row):
            columns_ref[tile, row : row + SUB, :] = value

        pack_columns(lambda field, z, row=row: load(field, z, row), depth, write)


def second_pack(first_ref, second_ref, own_ref, columns_ref, rows_ref):
    depth = rows_ref.shape[1]
    slots, _ = row_slots(depth)
    is_even = even("gx")
    sub = sublanes()
    tiles = {}
    for field, z, count, tile, start in slots:
        if tile not in tiles:
            first, second = first_ref[tile], second_ref[tile]
            tiles[tile] = (pick(is_even, second, first), pick(is_even, first, second))
        up, down = tiles[tile]
        before = turn(up, SUB - count - start, 0)
        after = turn(down, -start, 0)
        rows_ref[field, z] = jnp.where(sub < 4, after, before)
    own = own_ref.shape[1]
    columns_ref[:, :own, :] = own_ref[...]

    def write(tile, value):
        columns_ref[tile, own:, :] = value

    pack_columns(lambda field, z: rows_ref[field, z], depth, write)


def ahead(value, axis):
    return inner_coeff * (turn(value, -1, axis) - value) + outer_coeff * (
        turn(value, -2, axis) - turn(value, 1, axis)
    )


def behind(value, axis):
    return inner_coeff * (value - turn(value, 1, axis)) + outer_coeff * (
        turn(value, -1, axis) - turn(value, 2, axis)
    )


def depth_diff(plane, z, depth, offset):
    inside = lambda k: plane(k) if 0 <= k < depth else None

    def difference(high, low):
        if high is None:
            return None if low is None else -low
        return high if low is None else high - low

    near = difference(inside(z + 1 + offset), inside(z + offset))
    far = difference(inside(z + 2 + offset), inside(z - 1 + offset))
    total = inner_coeff * near
    return total if far is None else total + outer_coeff * far


def advance(
    forward_ref,
    adjoint_ref,
    pushed_ref,
    buoyancy_ref,
    rows_ref,
    first_ref,
    second_ref,
    terms_ref,
    moved_ref,
    rates_ref,
    field_ref,
    speed_ref,
):
    depth, rows, _ = buoyancy_ref.shape
    slot = column_slot_of()
    from_next = slot >= SLOT * SLOTS
    for place in range(SLOTS):
        from_next = from_next | ((slot >= SLOT * place + 3) & (slot < SLOT * place + 6))
    is_even = jnp.broadcast_to(even("gy"), (SUB, LANE))
    from_first = from_next == is_even
    merged = {}
    for k, (field, z) in enumerate(column_slots(depth)):
        if field == BUOYANCY:
            own = buoyancy_ref[z]
        elif field >= ADJOINT:
            own = adjoint_ref[0, field - ADJOINT, z]
        elif field < 3:
            own = pushed_ref[field, z]
        else:
            own = forward_ref[0, field, z]
        field_ref[field, z, :rows, :LANE] = own
        field_ref[field, z, rows:, :LANE] = rows_ref[field, z]
        tile, place = divmod(k, SLOTS)
        for row in range(0, RING, SUB):
            if (tile, row) not in merged:
                merged[tile, row] = jnp.where(
                    from_first,
                    first_ref[tile, row : row + SUB, :],
                    second_ref[tile, row : row + SUB, :],
                )
            field_ref[field, z, row : row + SUB, LANE:] = turn(
                merged[tile, row], -SLOT * place, 1
            )

    for base, step in ((0, advance_time_step), (ADJOINT, -advance_time_step)):
        for z in range(depth):
            get = lambda field: field_ref[base + field, z]
            along = lambda field, offset: depth_diff(
                lambda k: field_ref[base + field, k], z, depth, offset
            )
            scaled = step * field_ref[BUOYANCY, z]
            sxy, sxz, syz = get(SXY), get(SXZ), get(SYZ)
            speed_ref[base // 3, z] = get(VX) + scaled * (
                behind(get(SXX), 0) + ahead(sxy, 1) + along(SXZ, 0)
            )
            speed_ref[base // 3 + 1, z] = get(VY) + scaled * (
                ahead(sxy, 0) + behind(get(SYY), 1) + along(SYZ, 0)
            )
            speed_ref[base // 3 + 2, z] = get(VZ) + scaled * (
                ahead(sxz, 0) + ahead(syz, 1) + along(SZZ, -1)
            )

    for z in range(depth):
        rates = []
        for base in (0, 3):
            wide = lambda i: speed_ref[base + i, z, :rows, :]
            tall = lambda i: speed_ref[base + i, z, :, :LANE]
            along = lambda i, offset: depth_diff(
                lambda k: speed_ref[base + i, k, :rows, :LANE], z, depth, offset
            )
            over_x = lambda i, way: way(tall(i), 0)[:rows]
            over_y = lambda i, way: way(wide(i), 1)[:, :LANE]
            rates.append(
                (
                    over_x(0, ahead),
                    over_y(1, ahead),
                    along(2, 0),
                    over_y(0, behind) + over_x(1, behind),
                    along(0, -1) + over_x(2, behind),
                    along(1, -1) + over_y(2, behind),
                )
            )
        one, two = rates
        dilatation = one[0] + one[1] + one[2]
        other = two[0] + two[1] + two[2]
        for i in range(3):
            moved_ref[i, z] = speed_ref[i, z, :rows, :LANE]
        for i in range(6):
            rates_ref[i, z] = one[i]
        modulus = 2.0 * (one[0] * two[0] + one[1] * two[1] + one[2] * two[2])
        modulus = modulus + one[3] * two[3] + one[4] * two[4] + one[5] * two[5]
        density = sum(
            speed_ref[i, z, :rows, :LANE]
            * (speed_ref[3 + i, z, :rows, :LANE] - adjoint_ref[0, i, z])
            for i in range(3)
        )
        density = density / advance_time_step
        for copy in range(terms_ref.shape[0]):
            terms_ref[copy, 0, z] = dilatation * other
            terms_ref[copy, 1, z] = modulus
            terms_ref[copy, 2, z] = density


def advance_stress(forward_ref, lame_ref, shear_ref, moved_ref, rates_ref, next_ref):
    for z in range(lame_ref.shape[0]):
        shear = shear_ref[z]
        lame = lame_ref[z]
        dilatation = rates_ref[0, z] + rates_ref[1, z] + rates_ref[2, z]
        for i in range(3):
            next_ref[0, i, z] = moved_ref[i, z]
            next_ref[0, 3 + i, z] = forward_ref[0, 3 + i, z] + advance_time_step * (
                lame * dilatation + 2.0 * shear * rates_ref[i, z]
            )
            next_ref[0, 6 + i, z] = forward_ref[0, 6 + i, z] + advance_time_step * (
                shear * rates_ref[3 + i, z]
            )


def on_chip(kernel, out_shapes, scratch=(), cost=0, held=True):
    vmem = pl.BlockSpec(memory_space=pltpu.VMEM)
    space = pltpu.VMEM if held else pltpu.HBM
    place = lambda value: pltpu.with_memory_space_constraint(value, space)
    return lambda *operands: pl.pallas_call(
        kernel,
        out_shape=[pltpu.VMEM(shape, jnp.float32) for shape in out_shapes],
        in_specs=[vmem if held else pl.BlockSpec(memory_space=pl.ANY)] * len(operands),
        out_specs=[vmem] * len(out_shapes),
        scratch_shapes=list(scratch),
        cost_estimate=pl.CostEstimate(flops=cost, bytes_accessed=cost, transcendentals=0),
        compiler_params=pltpu.CompilerParams(vmem_limit_bytes=vmem_limit),
    )(*map(place, operands))


def swaps(devices, start):
    pairs = [(i, i + 1) for i in range(start, devices - 1, 2)]
    return pairs + [(j, i) for i, j in pairs]


def exchange(first, second, axis):
    devices = lax.axis_size(axis)
    return (
        lax.ppermute(first, axis, swaps(devices, 0)),
        lax.ppermute(second, axis, swaps(devices, 1)),
    )


def shards(
    forward_state,
    adjoint_state,
    first_lame_parameter,
    shear_stiffness,
    buoyancy,
    layer_mask,
    layer_element,
    layer_forces,
):
    depth, rows, lanes = buoyancy.shape
    events = lax.axis_size("ev")
    table = jnp.transpose(layer_forces, (1, 0, 2))
    tiles = row_slots(depth)[1]
    column_tiles = -(-depth * FIELDS // SLOTS)
    message = (tiles, SUB, lanes)
    state, plane = forward_state.shape, buoyancy.shape
    first, second, columns, pushed, forward_here, adjoint_here, buoyancy_here = on_chip(
        first_pack,
        [message, message, (column_tiles, rows, lanes), (3,) + plane, state, state, plane],
        [
            pltpu.VMEM(plane, jnp.int32),
            pltpu.VMEM(plane, jnp.int32),
            pltpu.VMEM(table.shape, jnp.float32),
            pltpu.SemaphoreType.DMA((6,)),
        ],
        cost=2_000_000,
        held=False,
    )(forward_state, adjoint_state, buoyancy, layer_mask, layer_element, table)
    first, second = exchange(first, second, "gx")
    columns, edge_rows = on_chip(
        second_pack,
        [(column_tiles, RING, lanes), (FIELDS, depth, SUB, lanes)],
        cost=1_000_000,
    )(first, second, columns)
    first, second = exchange(columns, columns, "gy")
    terms, moved, rates = on_chip(
        advance,
        [(events, 3) + plane, (3,) + plane, (6,) + plane],
        [
            pltpu.VMEM((FIELDS, depth, RING, 2 * lanes), jnp.float32),
            pltpu.VMEM((6, depth, RING, 2 * lanes), jnp.float32),
        ],
        cost=4_000_000,
    )(forward_here, adjoint_here, pushed, buoyancy_here, edge_rows, first, second)
    (forward_next,) = on_chip(advance_stress, [state], cost=2_000_000)(
        forward_here, first_lame_parameter, shear_stiffness, moved, rates
    )
    kernels = jnp.sum(lax.all_to_all(terms, "ev", 0, 0, tiled=True), axis=0)
    return (forward_next, kernels)


def solution(mesh):
    in_specs = (
        P("ev", None, None, "gx", "gy"),
        P("ev", None, None, "gx", "gy"),
        P(None, "gx", "gy"),
        P(None, "gx", "gy"),
        P(None, "gx", "gy"),
        P(None, "gx", "gy"),
        P(None, "gx", "gy"),
        P("ev", None, None),
    )
    out_specs = (P("ev", None, None, "gx", "gy"), P(None, None, "gx", "gy"))
    return jax.shard_map(shards, mesh=mesh, in_specs=in_specs, out_specs=out_specs, check_vma=False)
```

time: 316 us -> 44.7 us (0.14)
  the two profiles are of different devices: /device:TPU:32 before, /device:TPU:128 now
where the time goes in v2:
time: 44.7 us; the launch traced here: 44.4 us
  waiting for transfers between devices  20.7 us (46%)
  starting transfers between devices  17.9 us (40%)
  Pallas kernels  3.67 us (8%)
  local copies, waits for them, and re-layouts  0.72 us (2%)
  between operations  0.71 us (2%)
  other arithmetic  0.69 us (2%)
    all_to_all x1, waiting for transfers between devices, shards(): kernels = jnp.sum(lax.all_to_all(terms, 'ev', 0, 0, tiled=True), axis=0)  14.1 us
    ppermute x2, starting transfers between devices, exchange(): lax.ppermute(first, axis, swaps(devices, 0))  8.59 us
    all_to_all x1, starting transfers between devices, shards(): kernels = jnp.sum(lax.all_to_all(terms, 'ev', 0, 0, tiled=True), axis=0)  6.77 us
    ppermute x2, waiting for transfers between devices, exchange(): lax.ppermute(second, axis, swaps(devices, 1))  5.03 us
    pallas_call x4, Pallas kernels, on_chip(): pl.pallas_call(kernel, out_shape=[pltpu.VMEM(shape, jnp.float32) for shap...  3.67 us
    ppermute x2, starting transfers between devices, exchange(): lax.ppermute(second, axis, swaps(devices, 1))  2.58 us
    ppermute x2, waiting for transfers between devices, exchange(): lax.ppermute(first, axis, swaps(devices, 0))  1.52 us
  transfers between devices with their start and end apart: 5, of which 4 were waited for; matrix products, arithmetic and copies ran while one was open for 2% of the time, Pallas kernels for 0%

profile of v2, /device:TPU:128, one launch (start us, length us, event | category | flops | bytes accessed | tf_op | source)
XLA Modules:
  0.0 44.4 jit_solution(8921421689672010856)
XLA Ops:
  0.6 1.5 %shard_map.95 = (f32[22,8,128]{2,1,0:T(8,128)S(1)}, f32[22,8,128]{2,1,0:T(8,128)S(1)}, f32[4,16,128]{2,1,0:T(8,128)S(1)}, f32[3,4,16,128]{3,2,1,0:T(8,128)S(1)},...) custom-call(f32[1,9,4,16,128]{4,3,2,1,0:T(8,128)} %forward_hbm.1, ...), custom_call_target="tpu_custom_call" | custom-call | flops 2000000 | bytes 2000000 | tf_op jit(solution)/shard_map/pallas_call | solution.py:359
  2.1 3.8 %collective-permute-start = (f32[22,8,128]{2,1,0:T(8,128)S(1)}, f32[22,8,128]{2,1,0:T(8,128)S(1)}, u32[]{:S(2)}, u32[]{:S(2)}) collective-permute-start(f32[22,8,128]{2,1,0:T(8,128)S(1)} %get-tuple-element.18), channel_id=1, source_target_pairs={{0,4},{8,12},{16,20},{24,28},{32,36},{40,44},{48,52},{56,60},{4,0}... | collective-permute-start | bytes 270344 | tf_op jit(solution)/shard_map/ppermute | solution.py:378
  6.0 1.9 %collective-permute-start.1 = (f32[22,8,128]{2,1,0:T(8,128)S(1)}, f32[22,8,128]{2,1,0:T(8,128)S(1)}, u32[]{:S(2)}, u32[]{:S(2)}) collective-permute-start(f32[22,8,128]{2,1,0:T(8,128)S(1)} %get-tuple-element.19), channel_id=1, source_target_pairs={{4,8},{12,16},{20,24},{28,32},{36,40},{44,48},{52,56},{8,4},{16,12... | collective-permute-start | bytes 270344 | tf_op jit(solution)/shard_map/ppermute | solution.py:379
  7.9 0.7 %collective-permute-done.first_ref = f32[22,8,128]{2,1,0:T(8,128)S(1)} collective-permute-done((f32[22,8,128]{2,1,0:T(8,128)S(1)}, f32[22,8,128]{2,1,0:T(8,128)S(1)}, u32[]{:S(2)}, u32[]{:S(2)}) %collective-permute-start) | collective-permute-done | bytes 90144 | tf_op jit(solution)/shard_map/ppermute | solution.py:378
  8.6 5.0 %collective-permute-done.1.second_ref = f32[22,8,128]{2,1,0:T(8,128)S(1)} collective-permute-done((f32[22,8,128]{2,1,0:T(8,128)S(1)}, f32[22,8,128]{2,1,0:T(8,128)S(1)}, u32[]{:S(2)}, u32[]{:S(2)}) %collective-permute-start.1) | collective-permute-done | bytes 90144 | tf_op jit(solution)/shard_map/ppermute | solution.py:379
  13.6 0.2 shard_map.96
  13.8 0.7 %collective-permute-start.3 = (f32[4,24,128]{2,1,0:T(8,128)S(1)}, f32[4,24,128]{2,1,0:T(8,128)S(1)}, u32[]{:S(2)}, u32[]{:S(2)}) collective-permute-start(f32[4,24,128]{2,1,0:T(8,128)S(1)} %get-tuple-element.22), channel_id=1, source_target_pairs={{1,2},{2,1},{5,6},{6,5},{9,10},{10,9},{13,14},{14,13},{17,18},{18,... | collective-permute-start | bytes 147464 | tf_op jit(solution)/shard_map/ppermute | solution.py:379
  14.4 4.8 %collective-permute-start.2 = (f32[4,24,128]{2,1,0:T(8,128)S(1)}, f32[4,24,128]{2,1,0:T(8,128)S(1)}, u32[]{:S(2)}, u32[]{:S(2)}) collective-permute-start(f32[4,24,128]{2,1,0:T(8,128)S(1)} %get-tuple-element.22), channel_id=1, source_target_pairs={{0,1},{2,3},{1,0},{3,2},{4,5},{6,7},{5,4},{7,6},{8,9},{10,11},{9,8... | collective-permute-start | bytes 147464 | tf_op jit(solution)/shard_map/ppermute | solution.py:378
  19.2 0.0 collective-permute-done.3.second_ref
  19.2 0.8 %collective-permute-done.2.first_ref = f32[4,24,128]{2,1,0:T(8,128)S(1)} collective-permute-done((f32[4,24,128]{2,1,0:T(8,128)S(1)}, f32[4,24,128]{2,1,0:T(8,128)S(1)}, u32[]{:S(2)}, u32[]{:S(2)}) %collective-permute-start.2) | collective-permute-done | bytes 49184 | tf_op jit(solution)/shard_map/ppermute | solution.py:378
  20.1 2.0 %shard_map.97 = (f32[8,3,4,16,128]{4,3,2,1,0:T(8,128)}, f32[3,4,16,128]{3,2,1,0:T(8,128)S(1)}, f32[6,4,16,128]{3,2,1,0:T(8,128)S(1)}) custom-call(f32[1,9,4,16,128]{4,3,2,1,0:T(8,128)S(1)} %get-tuple-element.14.forward_ref, f32[1,9,4,16,128]{4,3,2,1,0:T(8,128)S(1)} %get-tuple-element.15.adjoint_ref, f32[3,4,16,128]{3,2,1,0:T(8,128)S(1)} %get-tuple-element.16.pushed_ref, ...), custom_call_target="tpu_custom_call" | custom-call | flops 4000000 | bytes 4000000 | tf_op jit(solution)/shard_map/pallas_call | solution.py:359
  22.0 0.0 copy-start
  22.0 0.0 copy-start.1
  22.1 6.8 %all-to-all-start = ((f32[8,3,4,16,128]{4,3,2,1,0:T(8,128)}), f32[8,3,4,16,128]{4,3,2,1,0:T(8,128)S(1)}, u32[]{:S(2)}, u32[]{:S(2)}) async-start(f32[8,3,4,16,128]{4,3,2,1,0:T(8,128)} %get-tuple-element.25), calls=%async_computation | async-start | bytes 1572864 | tf_op jit(solution)/shard_map/all_to_all | solution.py:431
  28.8 0.0 copy-done
  28.8 0.0 copy-done.1
  28.9 0.7 %copy.10 = f32[1,9,4,16,128]{4,3,2,1,0:T(8,128)} copy(f32[1,9,4,16,128]{4,3,2,1,0:T(8,128)S(1)} %shard_map.98) | data formatting | bytes 589824
  29.6 14.1 %all-to-all-done = f32[8,3,4,16,128]{4,3,2,1,0:T(8,128)S(1)} async-done(((f32[8,3,4,16,128]{4,3,2,1,0:T(8,128)}), f32[8,3,4,16,128]{4,3,2,1,0:T(8,128)S(1)}, u32[]{:S(2)}, u32[]{:S(2)}) %all-to-all-start) | async-done | bytes 786464 | tf_op jit(solution)/shard_map/all_to_all | solution.py:431
  43.7 0.7 %reduce_sum.9 = f32[3,4,16,128]{3,2,1,0:T(8,128)} reduce(f32[8,3,4,16,128]{4,3,2,1,0:T(8,128)S(1)} %all-to-all-done, f32[]{:T(128)} %constant.0.clone.1), dimensions={0}, to_apply=%region_0.0 | reduce | flops 172032 | bytes 884740 | tf_op jit(solution)/shard_map/reduce_sum | solution.py:431
  (1 shorter events, 0.0 us)
Async XLA Ops:
  2.1 6.4 %collective-permute-start = (f32[22,8,128]{2,1,0:T(8,128)S(1)}, f32[22,8,128]{2,1,0:T(8,128)S(1)}, u32[]{:S(2)}, u32[]{:S(2)}) collective-permute-start(f32[22,8,128]{2,1,0:T(8,128)S(1)} %get-tuple-element.18), channel_id=1, source_target_pairs={{0,4},{8,12},{16,20},{24,28},{32,36},{40,44},{48,52},{56,60},{4,0}... | collective-permute-start | bytes 270344 | tf_op jit(solution)/shard_map/ppermute | solution.py:378
  6.0 7.6 %collective-permute-start.1 = (f32[22,8,128]{2,1,0:T(8,128)S(1)}, f32[22,8,128]{2,1,0:T(8,128)S(1)}, u32[]{:S(2)}, u32[]{:S(2)}) collective-permute-start(f32[22,8,128]{2,1,0:T(8,128)S(1)} %get-tuple-element.19), channel_id=1, source_target_pairs={{4,8},{12,16},{20,24},{28,32},{36,40},{44,48},{52,56},{8,4},{16,12... | collective-permute-start | bytes 270344 | tf_op jit(solution)/shard_map/ppermute | solution.py:379
  13.8 5.4 %collective-permute-start.3 = (f32[4,24,128]{2,1,0:T(8,128)S(1)}, f32[4,24,128]{2,1,0:T(8,128)S(1)}, u32[]{:S(2)}, u32[]{:S(2)}) collective-permute-start(f32[4,24,128]{2,1,0:T(8,128)S(1)} %get-tuple-element.22), channel_id=1, source_target_pairs={{1,2},{2,1},{5,6},{6,5},{9,10},{10,9},{13,14},{14,13},{17,18},{18,... | collective-permute-start | bytes 147464 | tf_op jit(solution)/shard_map/ppermute | solution.py:379
  14.4 5.6 %collective-permute-start.2 = (f32[4,24,128]{2,1,0:T(8,128)S(1)}, f32[4,24,128]{2,1,0:T(8,128)S(1)}, u32[]{:S(2)}, u32[]{:S(2)}) collective-permute-start(f32[4,24,128]{2,1,0:T(8,128)S(1)} %get-tuple-element.22), channel_id=1, source_target_pairs={{0,1},{2,3},{1,0},{3,2},{4,5},{6,7},{5,4},{7,6},{8,9},{10,11},{9,8... | collective-permute-start | bytes 147464 | tf_op jit(solution)/shard_map/ppermute | solution.py:378
  22.0 6.8 %copy-start = (f32[4,16,128]{2,1,0:T(8,128)S(1)}, f32[4,16,128]{2,1,0:T(8,128)}, u32[]{:S(2)}) copy-start(f32[4,16,128]{2,1,0:T(8,128)} %lame_ref.1) | copy-start | bytes 98308
  22.0 6.8 %copy-start.1 = (f32[4,16,128]{2,1,0:T(8,128)S(1)}, f32[4,16,128]{2,1,0:T(8,128)}, u32[]{:S(2)}) copy-start(f32[4,16,128]{2,1,0:T(8,128)} %shear_ref.1) | copy-start | bytes 98308
  22.1 21.7 %all-to-all-start = ((f32[8,3,4,16,128]{4,3,2,1,0:T(8,128)}), f32[8,3,4,16,128]{4,3,2,1,0:T(8,128)S(1)}, u32[]{:S(2)}, u32[]{:S(2)}) async-start(f32[8,3,4,16,128]{4,3,2,1,0:T(8,128)} %get-tuple-element.25), calls=%async_computation | async-start | bytes 1572864 | tf_op jit(solution)/shard_map/all_to_all | solution.py:431

commit v3 on v2

v3 whole, which is shorter than its diff:
```python
import functools

import jax
import jax.numpy as jnp
from jax import lax
from jax.experimental import pallas as pl
from jax.experimental.pallas import tpu as pltpu
from jax.sharding import PartitionSpec as P

inner_coeff = 9.0 / 8.0
outer_coeff = -1.0 / 24.0
ratio = outer_coeff / inner_coeff
advance_time_step = 0.15
vmem_limit = 16 << 20

PX, PY, PZ, SXX, SYY, SXY, SXZ, SYZ = range(8)
ADJOINT = 8
BUOYANCY = 16
FIELDS = 17
STATE_SLOT = {SXX: 3, SYY: 4, SXY: 6, SXZ: 7, SYZ: 8}
ALONG_X = (SXX, SXY, SXZ)
SUB, LANE = 8, 128
RING = 24
SLOT = 6
SLOTS = 21


def row_slots(depth):
    three = [
        (base + field, z) for z in range(depth) for base in (0, ADJOINT) for field in ALONG_X
    ]
    two = [
        (field, z)
        for z in range(depth)
        for field in range(FIELDS)
        if field == BUOYANCY or field % ADJOINT not in ALONG_X
    ]
    slots, tile, sub = [], 0, 0
    while three or two:
        if three and sub <= 3:
            (field, z), rows = three.pop(0), 3
        else:
            (field, z), rows = two.pop(0), 2
        slots.append((field, z, rows, tile, sub))
        sub += rows
        if sub + 2 > SUB:
            tile, sub = tile + 1, 0
    return slots, tile + (sub > 0)


def column_slots(depth):
    return [(field, z) for z in range(depth) for field in range(FIELDS)]


def turn(value, amount, axis):
    amount %= value.shape[axis]
    return pltpu.roll(value, amount, axis) if amount else value


def sublanes():
    return lax.broadcasted_iota(jnp.int32, (SUB, LANE), 0)


def column_slot_of():
    return jnp.bitwise_and(lax.broadcasted_iota(jnp.int32, (SUB, LANE), 1) + 3, LANE - 1)


def even(axis):
    return jnp.bitwise_and(lax.axis_index(axis), 1) == 0


def pick(condition, first, second):
    return jnp.where(jnp.broadcast_to(condition, first.shape), first, second)


def lookup(mask_ref, element_ref, table_ref, z, row):
    element = element_ref[z, row : row + SUB, :]
    weight = mask_ref[z, row : row + SUB, :].astype(jnp.float32)
    lane = jnp.bitwise_and(element, LANE - 1)
    part = jnp.right_shift(element, 7)
    parts = table_ref.shape[2] // LANE
    found = []
    for first in range(3):
        value = None
        for k in range(parts):
            part_lanes = slice(LANE * k, LANE * (k + 1))
            entries = jnp.broadcast_to(table_ref[first, :, part_lanes], (SUB, LANE))
            taken = jnp.take_along_axis(entries, lane, axis=1, mode="promise_in_bounds")
            value = taken if k == 0 else jnp.where(part == k, taken, value)
        found.append(weight * value)
    return found


def pack_columns(load, depth, write):
    slot = column_slot_of()
    value = None
    slots = column_slots(depth)
    for k, (field, z) in enumerate(slots):
        tile, place = divmod(k, SLOTS)
        moved = turn(load(field, z), SLOT * place, 1)
        if place == 0:
            value = moved
        else:
            value = jnp.where(slot >= SLOT * place, moved, value)
        if place == SLOTS - 1 or k == len(slots) - 1:
            write(tile, value)


def depth_diff(plane, z, depth, offset):
    inside = lambda k: plane(k) if 0 <= k < depth else None

    def difference(high, low):
        if high is None:
            return None if low is None else -low
        return high if low is None else high - low

    near = difference(inside(z + 1 + offset), inside(z + offset))
    far = difference(inside(z + 2 + offset), inside(z - 1 + offset))
    return near if far is None else near + ratio * far


def own_tile(pushed_ref, forward_ref, adjoint_ref, buoyancy_ref, field, z, row):
    rows = slice(row, row + SUB)
    if field == BUOYANCY:
        return buoyancy_ref[z, rows, :]
    adjoint, field = divmod(field, ADJOINT)
    if field <= PZ:
        return pushed_ref[3 * adjoint + field, z, rows, :]
    return (adjoint_ref if adjoint else forward_ref)[0, STATE_SLOT[field], z, rows, :]


def first_pack(
    forward_hbm,
    adjoint_hbm,
    buoyancy_hbm,
    mask_hbm,
    element_hbm,
    table_hbm,
    first_ref,
    second_ref,
    pushed_ref,
    forward_ref,
    adjoint_ref,
    buoyancy_ref,
    mask_ref,
    element_ref,
    table_ref,
    arrivals,
):
    depth, rows, _ = buoyancy_ref.shape
    loads = [
        pltpu.make_async_copy(source, target, arrivals.at[k])
        for k, (source, target) in enumerate(
            (
                (element_hbm, element_ref),
                (mask_hbm, mask_ref),
                (table_hbm, table_ref),
                (buoyancy_hbm, buoyancy_ref),
                (forward_hbm, forward_ref),
                (adjoint_hbm, adjoint_ref),
            )
        )
    ]
    for copy in loads:
        copy.start()
    for copy in loads[:3]:
        copy.wait()
    cells = [(z, row) for z in range(depth) for row in range(0, rows, SUB)]
    for z, row in cells:
        for i, forcing in enumerate(lookup(mask_ref, element_ref, table_ref, z, row)):
            pushed_ref[i, z, row : row + SUB, :] = advance_time_step * forcing
    loads[3].wait()
    for state_ref, copy, base, step in (
        (forward_ref, loads[4], 0, advance_time_step),
        (adjoint_ref, loads[5], 3, -advance_time_step),
    ):
        copy.wait()
        for z, row in cells:
            part = slice(row, row + SUB)
            scaled = (step * inner_coeff) * buoyancy_ref[z, part, :]
            for i, (field, offset) in enumerate(((7, 0), (8, 0), (5, -1))):
                along = depth_diff(lambda k: state_ref[0, field, k, part, :], z, depth, offset)
                value = state_ref[0, i, z, part, :] + scaled * along
                if base == 0:
                    value = value + pushed_ref[i, z, part, :]
                pushed_ref[base + i, z, part, :] = value

    load = functools.partial(own_tile, pushed_ref, forward_ref, adjoint_ref, buoyancy_ref)
    slots, tiles = row_slots(depth)
    sub = sublanes()
    is_even = even("gx")
    for tile in range(tiles):
        up, down = None, None
        for field, z, count, at, start in slots:
            if at != tile:
                continue
            last = turn(load(field, z, rows - SUB), start + count, 0)
            first = turn(load(field, z, 0), start, 0)
            up = last if up is None else jnp.where(sub >= start, last, up)
            down = first if down is None else jnp.where(sub >= start, first, down)
        first_ref[tile] = pick(is_even, up, down)
        second_ref[tile] = pick(is_even, down, up)


def own_columns(pushed_ref, forward_ref, adjoint_ref, buoyancy_ref, columns_ref):
    depth, rows, _ = buoyancy_ref.shape
    load = functools.partial(own_tile, pushed_ref, forward_ref, adjoint_ref, buoyancy_ref)
    for row in range(0, rows, SUB):

        def write(tile, value, row=row):
            columns_ref[tile, row : row + SUB, :] = value

        pack_columns(lambda field, z, row=row: load(field, z, row), depth, write)


def second_pack(first_ref, second_ref, own_ref, columns_ref, rows_ref):
    depth = rows_ref.shape[1]
    slots, _ = row_slots(depth)
    is_even = even("gx")
    sub = sublanes()
    tiles = {}
    for field, z, count, tile, start in slots:
        if tile not in tiles:
            first, second = first_ref[tile], second_ref[tile]
            tiles[tile] = (pick(is_even, second, first), pick(is_even, first, second))
        up, down = tiles[tile]
        before = turn(up, SUB - count - start, 0)
        after = turn(down, -start, 0)
        rows_ref[field, z] = jnp.where(sub < 4, after, before)
    own = own_ref.shape[1]
    columns_ref[:, :own, :] = own_ref[...]

    def write(tile, value):
        columns_ref[tile, own:, :] = value

    pack_columns(lambda field, z: rows_ref[field, z], depth, write)


def ahead(value, axis):
    return (turn(value, -1, axis) - value) + ratio * (turn(value, -2, axis) - turn(value, 1, axis))


def behind(value, axis):
    return (value - turn(value, 1, axis)) + ratio * (turn(value, -1, axis) - turn(value, 2, axis))


def advance(
    forward_ref,
    adjoint_ref,
    pushed_ref,
    buoyancy_ref,
    rows_ref,
    first_ref,
    second_ref,
    terms_ref,
    moved_ref,
    rates_ref,
    field_ref,
    speed_ref,
):
    depth, rows, _ = buoyancy_ref.shape
    load = functools.partial(own_tile, pushed_ref, forward_ref, adjoint_ref, buoyancy_ref)
    slot = column_slot_of()
    from_next = slot >= SLOT * SLOTS
    for place in range(SLOTS):
        from_next = from_next | ((slot >= SLOT * place + 3) & (slot < SLOT * place + 6))
    from_first = from_next == jnp.broadcast_to(even("gy"), (SUB, LANE))
    merged = {}
    for k, (field, z) in enumerate(column_slots(depth)):
        tile, place = divmod(k, SLOTS)
        for row in range(0, RING, SUB):
            part = slice(row, row + SUB)
            field_ref[field, z, part, :LANE] = (
                load(field, z, row) if row < rows else rows_ref[field, z]
            )
            if (tile, row) not in merged:
                merged[tile, row] = jnp.where(
                    from_first, first_ref[tile, part, :], second_ref[tile, part, :]
                )
            field_ref[field, z, part, LANE:] = turn(merged[tile, row], -SLOT * place, 1)

    for state, step in ((0, advance_time_step), (1, -advance_time_step)):
        for z in range(depth):
            get = lambda field: field_ref[state * ADJOINT + field, z]
            scaled = (step * inner_coeff) * field_ref[BUOYANCY, z]
            sxy = get(SXY)
            changes = (
                behind(get(SXX), 0) + ahead(sxy, 1),
                ahead(sxy, 0) + behind(get(SYY), 1),
                ahead(get(SXZ), 0) + ahead(get(SYZ), 1),
            )
            for i, change in enumerate(changes):
                speed_ref[3 * state + i, z] = get(i) + scaled * change

    for z in range(depth):
        rates = []
        for base in (0, 3):
            along = lambda i, offset: depth_diff(
                lambda k: speed_ref[base + i, k, :rows, :LANE], z, depth, offset
            )
            over_x = lambda i, way: way(speed_ref[base + i, z, :, :LANE], 0)[:rows]
            over_y = lambda i, way: way(speed_ref[base + i, z, :rows, :], 1)[:, :LANE]
            rates.append(
                (
                    over_x(0, ahead),
                    over_y(1, ahead),
                    along(2, 0),
                    over_y(0, behind) + over_x(1, behind),
                    along(0, -1) + over_x(2, behind),
                    along(1, -1) + over_y(2, behind),
                )
            )
        one, two = rates
        first_invariant = (one[0] + one[1] + one[2]) * (two[0] + two[1] + two[2])
        modulus = 2.0 * (one[0] * two[0] + one[1] * two[1] + one[2] * two[2])
        modulus = modulus + one[3] * two[3] + one[4] * two[4] + one[5] * two[5]
        density = None
        for i in range(3):
            moved = speed_ref[i, z, :rows, :LANE]
            moved_ref[i, z] = moved
            gain = moved * (speed_ref[3 + i, z, :rows, :LANE] - adjoint_ref[0, i, z])
            density = gain if density is None else density + gain
        for i in range(6):
            rates_ref[i, z] = one[i]
        terms_ref[0, z] = (inner_coeff * inner_coeff) * first_invariant
        terms_ref[1, z] = (inner_coeff * inner_coeff) * modulus
        terms_ref[2, z] = density / advance_time_step


def advance_stress(
    forward_ref, lame_ref, shear_ref, moved_ref, rates_ref, next_hbm, next_ref, leaves
):
    step = advance_time_step * inner_coeff
    for z in range(lame_ref.shape[0]):
        shear = step * shear_ref[z]
        dilatation = rates_ref[0, z] + rates_ref[1, z] + rates_ref[2, z]
        pressure = step * lame_ref[z] * dilatation
        for i in range(3):
            next_ref[0, i, z] = moved_ref[i, z]
            next_ref[0, 3 + i, z] = forward_ref[0, 3 + i, z] + (
                pressure + 2.0 * shear * rates_ref[i, z]
            )
            next_ref[0, 6 + i, z] = forward_ref[0, 6 + i, z] + shear * rates_ref[3 + i, z]
    copy = pltpu.make_async_copy(next_ref, next_hbm, leaves)
    copy.start()
    copy.wait()


def add_pair(one_ref, two_ref, _, sum_ref):
    total = one_ref[...] + two_ref[...]
    for copy in range(sum_ref.shape[0]):
        sum_ref[copy] = total


def on_chip(kernel, out_shapes, scratch=(), cost=0, far=(), away=()):
    vmem, anywhere = [pl.BlockSpec(memory_space=space) for space in (pltpu.VMEM, pl.ANY)]
    place = lambda k, value: pltpu.with_memory_space_constraint(
        value, pltpu.HBM if k in far else pltpu.VMEM
    )
    return lambda *operands: pl.pallas_call(
        kernel,
        out_shape=[
            (pltpu.HBM if k in away else pltpu.VMEM)(shape, jnp.float32)
            for k, shape in enumerate(out_shapes)
        ],
        in_specs=[anywhere if k in far else vmem for k in range(len(operands))],
        out_specs=[anywhere if k in away else vmem for k in range(len(out_shapes))],
        scratch_shapes=list(scratch),
        cost_estimate=pl.CostEstimate(flops=cost, bytes_accessed=cost, transcendentals=0),
        compiler_params=pltpu.CompilerParams(vmem_limit_bytes=vmem_limit),
    )(*[place(k, value) for k, value in enumerate(operands)])


def swaps(devices, start):
    pairs = [(i, i + 1) for i in range(start, devices - 1, 2)]
    return pairs + [(j, i) for i, j in pairs]


def exchange(first, second, axis):
    devices = lax.axis_size(axis)
    return (
        lax.ppermute(first, axis, swaps(devices, 0)),
        lax.ppermute(second, axis, swaps(devices, 1)),
    )


def shards(
    forward_state,
    adjoint_state,
    first_lame_parameter,
    shear_stiffness,
    buoyancy,
    layer_mask,
    layer_element,
    layer_forces,
):
    depth, rows, lanes = buoyancy.shape
    events = lax.axis_size("ev")
    table = jnp.transpose(layer_forces, (1, 0, 2))
    tiles = row_slots(depth)[1]
    column_tiles = -(-depth * FIELDS // SLOTS)
    message = (tiles, SUB, lanes)
    state, plane = forward_state.shape, buoyancy.shape
    first, second, pushed, forward_here, adjoint_here, buoyancy_here = on_chip(
        first_pack,
        [message, message, (6,) + plane, state, state, plane],
        [
            pltpu.VMEM(plane, jnp.int32),
            pltpu.VMEM(plane, jnp.int32),
            pltpu.VMEM(table.shape, jnp.float32),
            pltpu.SemaphoreType.DMA((6,)),
        ],
        cost=2_000_000,
        far=range(6),
    )(forward_state, adjoint_state, buoyancy, layer_mask, layer_element, table)
    first, second = exchange(first, second, "gx")
    (columns,) = on_chip(own_columns, [(column_tiles, rows, lanes)], cost=1_000_000)(
        pushed, forward_here, adjoint_here, buoyancy_here
    )
    columns, edge_rows = on_chip(
        second_pack,
        [(column_tiles, RING, lanes), (FIELDS, depth, SUB, lanes)],
        cost=1_000_000,
    )(first, second, columns)
    first, second = exchange(columns, columns, "gy")
    terms, moved, rates = on_chip(
        advance,
        [(3,) + plane, (3,) + plane, (6,) + plane],
        [
            pltpu.VMEM((FIELDS, depth, RING, 2 * lanes), jnp.float32),
            pltpu.VMEM((6, depth, RING, 2 * lanes), jnp.float32),
        ],
        cost=4_000_000,
    )(forward_here, adjoint_here, pushed, buoyancy_here, edge_rows, first, second)
    partner = lax.ppermute(terms, "ev", [(i, i ^ 1) for i in range(events)])
    (forward_next,) = on_chip(
        advance_stress,
        [state],
        [pltpu.VMEM(state, jnp.float32), pltpu.SemaphoreType.DMA(())],
        cost=2_000_000,
        away=(0,),
    )(
        forward_here, first_lame_parameter, shear_stiffness, moved, rates
    )
    (pairs,) = on_chip(add_pair, [(events // 2, 3) + plane], cost=500_000, far=(2,))(
        terms, partner, forward_next
    )
    groups = [list(range(k, events, 2)) for k in range(2)]
    kernels = jnp.sum(
        lax.all_to_all(pairs, "ev", 0, 0, axis_index_groups=groups, tiled=True), axis=0
    )
    return (forward_next, kernels)


def solution(mesh):
    in_specs = (
        P("ev", None, None, "gx", "gy"),
        P("ev", None, None, "gx", "gy"),
        P(None, "gx", "gy"),
        P(None, "gx", "gy"),
        P(None, "gx", "gy"),
        P(None, "gx", "gy"),
        P(None, "gx", "gy"),
        P("ev", None, None),
    )
    out_specs = (P("ev", None, None, "gx", "gy"), P(None, None, "gx", "gy"))
    return jax.shard_map(shards, mesh=mesh, in_specs=in_specs, out_specs=out_specs, check_vma=False)
```

time: 44.7 us -> 42.2 us (0.944)
  blocking collectives: 0 us -> 12 us
  waiting for transfers between devices: 20.7 us -> 9.28 us
  starting transfers between devices: 17.9 us -> 15.8 us
  local copies, waits for them, and re-layouts: 0.72 us -> 0.01 us
    all_to_all x1 -> x0, waiting for transfers between devices: 14.1 us -> none  [shards(): kernels = jnp.sum(lax.all_to_all(terms, 'ev', 0, 0, tiled=True), axis=0)]
    all_to_all x0 -> x1, blocking collectives: none -> 12 us  [shards(): lax.all_to_all(pairs, 'ev', 0, 0, axis_index_groups=groups, tiled=True)]
    all_to_all x1 -> x0, starting transfers between devices: 6.77 us -> none  [shards(): kernels = jnp.sum(lax.all_to_all(terms, 'ev', 0, 0, tiled=True), axis=0)]
    ppermute x0 -> x1, starting transfers between devices: none -> 4.64 us  [shards(): partner = lax.ppermute(terms, 'ev', [(i, i ^ 1) for i in range(events)])]
    ppermute x0 -> x1, waiting for transfers between devices: none -> 3.02 us  [shards(): partner = lax.ppermute(terms, 'ev', [(i, i ^ 1) for i in range(events)])]
    unnamed x5 -> x4, local copies, waits for them, and re-layouts: 0.72 us -> 0.01 us
    pallas_call x4 -> x6, Pallas kernels: 3.67 us -> 3.39 us  [on_chip(): pl.pallas_call(kernel, out_shape=[(pltpu.HBM if k in away else pltpu.VMEM...]
  transfers between devices with their start and end apart: 5 -> 5, of which waited for: 4 -> 4; matrix products, arithmetic and copies ran while one was open for 2% -> 0% of each run, Pallas kernels for 0% -> 2%
where the time goes in v3:
time: 42.2 us; the launch traced here: 41.9 us
  starting transfers between devices  15.8 us (37%)
  blocking collectives  12 us (28%)
  waiting for transfers between devices  9.28 us (22%)
  Pallas kernels  3.39 us (8%)
  between operations  0.74 us (2%)
  other arithmetic  0.67 us (2%)
    all_to_all x1, blocking collectives, shards(): lax.all_to_all(pairs, 'ev', 0, 0, axis_index_groups=groups, tiled=True)  12 us
    ppermute x2, starting transfers between devices, exchange(): lax.ppermute(first, axis, swaps(devices, 0))  8.59 us
    ppermute x2, waiting for transfers between devices, exchange(): lax.ppermute(second, axis, swaps(devices, 1))  5.05 us
    ppermute x1, starting transfers between devices, shards(): partner = lax.ppermute(terms, 'ev', [(i, i ^ 1) for i in range(events)])  4.64 us
    pallas_call x6, Pallas kernels, on_chip(): pl.pallas_call(kernel, out_shape=[(pltpu.HBM if k in away else pltpu.VMEM...  3.39 us
    ppermute x1, waiting for transfers between devices, shards(): partner = lax.ppermute(terms, 'ev', [(i, i ^ 1) for i in range(events)])  3.02 us
    ppermute x2, starting transfers between devices, exchange(): lax.ppermute(second, axis, swaps(devices, 1))  2.58 us
    ppermute x2, waiting for transfers between devices, exchange(): lax.ppermute(first, axis, swaps(devices, 0))  1.22 us
  transfers between devices with their start and end apart: 5, of which 4 were waited for; matrix products, arithmetic and copies ran while one was open for 0% of the time, Pallas kernels for 2%

profile of v3, /device:TPU:128, one launch (start us, length us, event | category | flops | bytes accessed | tf_op | source)
XLA Modules:
  0.0 41.9 jit_solution(16320505768908724156)
XLA Ops:
  0.6 1.2 %shard_map.95 = (f32[20,8,128]{2,1,0:T(8,128)S(1)}, f32[20,8,128]{2,1,0:T(8,128)S(1)}, f32[6,4,16,128]{3,2,1,0:T(8,128)S(1)}, f32[1,9,4,16,128]{4,3,2,1,0:T(8,12...) custom-call(f32[1,9,4,16,128]{4,3,2,1,0:T(8,128)} %forward_hbm.1, ...), custom_call_target="tpu_custom_call" | custom-call | flops 2000000 | bytes 2000000 | tf_op jit(solution)/shard_map/pallas_call | solution.py:360
  1.9 3.8 %collective-permute-start = (f32[20,8,128]{2,1,0:T(8,128)S(1)}, f32[20,8,128]{2,1,0:T(8,128)S(1)}, u32[]{:S(2)}, u32[]{:S(2)}) collective-permute-start(f32[20,8,128]{2,1,0:T(8,128)S(1)} %get-tuple-element.17), channel_id=1, source_target_pairs={{0,4},{8,12},{16,20},{24,28},{32,36},{40,44},{48,52},{56,60},{4,0}... | collective-permute-start | bytes 245768 | tf_op jit(solution)/shard_map/ppermute | solution.py:382
  5.7 1.9 %collective-permute-start.1 = (f32[20,8,128]{2,1,0:T(8,128)S(1)}, f32[20,8,128]{2,1,0:T(8,128)S(1)}, u32[]{:S(2)}, u32[]{:S(2)}) collective-permute-start(f32[20,8,128]{2,1,0:T(8,128)S(1)} %get-tuple-element.18), channel_id=1, source_target_pairs={{4,8},{12,16},{20,24},{28,32},{36,40},{44,48},{52,56},{8,4},{16,12... | collective-permute-start | bytes 245768 | tf_op jit(solution)/shard_map/ppermute | solution.py:383
  7.6 0.2 shard_map.96.own_ref
  7.8 0.4 collective-permute-done.first_ref
  8.2 5.0 %collective-permute-done.1.second_ref = f32[20,8,128]{2,1,0:T(8,128)S(1)} collective-permute-done((f32[20,8,128]{2,1,0:T(8,128)S(1)}, f32[20,8,128]{2,1,0:T(8,128)S(1)}, u32[]{:S(2)}, u32[]{:S(2)}) %collective-permute-start.1) | collective-permute-done | bytes 81952 | tf_op jit(solution)/shard_map/ppermute | solution.py:383
  13.3 0.1 shard_map.97
  13.4 0.7 %collective-permute-start.3 = (f32[4,24,128]{2,1,0:T(8,128)S(1)}, f32[4,24,128]{2,1,0:T(8,128)S(1)}, u32[]{:S(2)}, u32[]{:S(2)}) collective-permute-start(f32[4,24,128]{2,1,0:T(8,128)S(1)} %get-tuple-element.20), channel_id=1, source_target_pairs={{1,2},{2,1},{5,6},{6,5},{9,10},{10,9},{13,14},{14,13},{17,18},{18,... | collective-permute-start | bytes 147464 | tf_op jit(solution)/shard_map/ppermute | solution.py:383
  14.1 4.8 %collective-permute-start.2 = (f32[4,24,128]{2,1,0:T(8,128)S(1)}, f32[4,24,128]{2,1,0:T(8,128)S(1)}, u32[]{:S(2)}, u32[]{:S(2)}) collective-permute-start(f32[4,24,128]{2,1,0:T(8,128)S(1)} %get-tuple-element.20), channel_id=1, source_target_pairs={{0,1},{2,3},{1,0},{3,2},{4,5},{6,7},{5,4},{7,6},{8,9},{10,11},{9,8... | collective-permute-start | bytes 147464 | tf_op jit(solution)/shard_map/ppermute | solution.py:382
  18.8 0.0 collective-permute-done.3.second_ref
  18.8 0.8 %collective-permute-done.2.first_ref = f32[4,24,128]{2,1,0:T(8,128)S(1)} collective-permute-done((f32[4,24,128]{2,1,0:T(8,128)S(1)}, f32[4,24,128]{2,1,0:T(8,128)S(1)}, u32[]{:S(2)}, u32[]{:S(2)}) %collective-permute-start.2) | collective-permute-done | bytes 49184 | tf_op jit(solution)/shard_map/ppermute | solution.py:382
  19.7 0.0 copy-start
  19.7 0.0 copy-start.1
  19.7 1.0 %shard_map.98 = (f32[3,4,16,128]{3,2,1,0:T(8,128)S(1)}, f32[3,4,16,128]{3,2,1,0:T(8,128)S(1)}, f32[6,4,16,128]{3,2,1,0:T(8,128)S(1)}) custom-call(f32[1,9,4,16,128]{4,3,2,1,0:T(8,128)S(1)} %get-tuple-element.13.forward_ref, f32[1,9,4,16,128]{4,3,2,1,0:T(8,128)S(1)} %get-tuple-element.14.adjoint_ref, f32[6,4,16,128]{3,2,1,0:T(8,128)S(1)} %get-tuple-element.15.pushed_ref, ...), custom_call_target="tpu_custom_call" | custom-call | flops 4000000 | bytes 4000000 | tf_op jit(solution)/shard_map/pallas_call | solution.py:360
  20.7 4.6 %collective-permute-start.4 = (f32[3,4,16,128]{3,2,1,0:T(8,128)S(1)}, f32[3,4,16,128]{3,2,1,0:T(8,128)S(1)}, u32[]{:S(2)}, u32[]{:S(2)}) collective-permute-start(f32[3,4,16,128]{3,2,1,0:T(8,128)S(1)} %get-tuple-element.23.one_ref), channel_id=1, source_target_pairs={{0,64},{64,0},{128,192},{192,128},{256,320},{320,256},{384,448},{4... | collective-permute-start | bytes 294920 | tf_op jit(solution)/shard_map/ppermute | solution.py:435
  25.4 0.0 copy-done
  25.4 0.0 copy-done.1
  25.4 0.8 %shard_map.99._ = f32[1,9,4,16,128]{4,3,2,1,0:T(8,128)} custom-call(f32[1,9,4,16,128]{4,3,2,1,0:T(8,128)S(1)} %get-tuple-element.13.forward_ref, f32[4,16,128]{2,1,0:T(8,128)S(1)} %copy-done, f32[4,16,128]{2,1,0:T(8,128)S(1)} %copy-done.1, f32[3,4,16,128]{3,2,1,0:T(8,128)S(1)} %get-tuple-element.21.moved_ref, f32[6,4,16,128]{3,2,1,0:T(8,128)S(1)} %get-tuple-element.22.rates_ref), custom_call_target="tpu_custom_call" | custom-call | flops 2000000 | bytes 2000000 | tf_op jit(solution)/shard_map/pallas_call | solution.py:360
  26.2 3.0 %collective-permute-done.4.two_ref = f32[3,4,16,128]{3,2,1,0:T(8,128)S(1)} collective-permute-done((f32[3,4,16,128]{3,2,1,0:T(8,128)S(1)}, f32[3,4,16,128]{3,2,1,0:T(8,128)S(1)}, u32[]{:S(2)}, u32[]{:S(2)}) %collective-permute-start.4) | collective-permute-done | bytes 98336 | tf_op jit(solution)/shard_map/ppermute | solution.py:435
  29.2 12.0 %all_to_all.5 = f32[4,3,4,16,128]{4,3,2,1,0:T(8,128)S(1)} all-to-all(f32[4,3,4,16,128]{4,3,2,1,0:T(8,128)S(1)} %shard_map.100), channel_id=1, replica_groups={{0,128,256,384},{64,192,320,448},{1,129,257,385},{65,193,321,449},{2,13..., dimensions={0} | all-to-all | bytes 786432 | tf_op jit(solution)/shard_map/all_to_all | solution.py:450
  41.2 0.7 %reduce_sum.9 = f32[3,4,16,128]{3,2,1,0:T(8,128)} reduce(f32[4,3,4,16,128]{4,3,2,1,0:T(8,128)S(1)} %all_to_all.5, f32[]{:T(128)} %constant.0.clone.1), dimensions={0}, to_apply=%region_0.0 | reduce | flops 73728 | bytes 491524 | tf_op jit(solution)/shard_map/reduce_sum | solution.py:449
  (1 shorter events, 0.0 us)
Async XLA Ops:
  1.9 6.3 %collective-permute-start = (f32[20,8,128]{2,1,0:T(8,128)S(1)}, f32[20,8,128]{2,1,0:T(8,128)S(1)}, u32[]{:S(2)}, u32[]{:S(2)}) collective-permute-start(f32[20,8,128]{2,1,0:T(8,128)S(1)} %get-tuple-element.17), channel_id=1, source_target_pairs={{0,4},{8,12},{16,20},{24,28},{32,36},{40,44},{48,52},{56,60},{4,0}... | collective-permute-start | bytes 245768 | tf_op jit(solution)/shard_map/ppermute | solution.py:382
  5.7 7.5 %collective-permute-start.1 = (f32[20,8,128]{2,1,0:T(8,128)S(1)}, f32[20,8,128]{2,1,0:T(8,128)S(1)}, u32[]{:S(2)}, u32[]{:S(2)}) collective-permute-start(f32[20,8,128]{2,1,0:T(8,128)S(1)} %get-tuple-element.18), channel_id=1, source_target_pairs={{4,8},{12,16},{20,24},{28,32},{36,40},{44,48},{52,56},{8,4},{16,12... | collective-permute-start | bytes 245768 | tf_op jit(solution)/shard_map/ppermute | solution.py:383
  13.4 5.4 %collective-permute-start.3 = (f32[4,24,128]{2,1,0:T(8,128)S(1)}, f32[4,24,128]{2,1,0:T(8,128)S(1)}, u32[]{:S(2)}, u32[]{:S(2)}) collective-permute-start(f32[4,24,128]{2,1,0:T(8,128)S(1)} %get-tuple-element.20), channel_id=1, source_target_pairs={{1,2},{2,1},{5,6},{6,5},{9,10},{10,9},{13,14},{14,13},{17,18},{18,... | collective-permute-start | bytes 147464 | tf_op jit(solution)/shard_map/ppermute | solution.py:383
  14.1 5.6 %collective-permute-start.2 = (f32[4,24,128]{2,1,0:T(8,128)S(1)}, f32[4,24,128]{2,1,0:T(8,128)S(1)}, u32[]{:S(2)}, u32[]{:S(2)}) collective-permute-start(f32[4,24,128]{2,1,0:T(8,128)S(1)} %get-tuple-element.20), channel_id=1, source_target_pairs={{0,1},{2,3},{1,0},{3,2},{4,5},{6,7},{5,4},{7,6},{8,9},{10,11},{9,8... | collective-permute-start | bytes 147464 | tf_op jit(solution)/shard_map/ppermute | solution.py:382
  19.7 5.7 %copy-start = (f32[4,16,128]{2,1,0:T(8,128)S(1)}, f32[4,16,128]{2,1,0:T(8,128)}, u32[]{:S(2)}) copy-start(f32[4,16,128]{2,1,0:T(8,128)} %lame_ref.1) | copy-start | bytes 98308
  19.7 5.7 %copy-start.1 = (f32[4,16,128]{2,1,0:T(8,128)S(1)}, f32[4,16,128]{2,1,0:T(8,128)}, u32[]{:S(2)}) copy-start(f32[4,16,128]{2,1,0:T(8,128)} %shear_ref.1) | copy-start | bytes 98308
  20.7 8.4 %collective-permute-start.4 = (f32[3,4,16,128]{3,2,1,0:T(8,128)S(1)}, f32[3,4,16,128]{3,2,1,0:T(8,128)S(1)}, u32[]{:S(2)}, u32[]{:S(2)}) collective-permute-start(f32[3,4,16,128]{3,2,1,0:T(8,128)S(1)} %get-tuple-element.23.one_ref), channel_id=1, source_target_pairs={{0,64},{64,0},{128,192},{192,128},{256,320},{320,256},{384,448},{4... | collective-permute-start | bytes 294920 | tf_op jit(solution)/shard_map/ppermute | solution.py:435

commit v4 on v3

--- a/solution.py
+++ b/solution.py
@@ -244,6 +244,25 @@
     return (value - turn(value, 1, axis)) + ratio * (turn(value, -1, axis) - turn(value, 2, axis))
 
 
+def crossing(here, there):
+    lane = lax.broadcasted_iota(jnp.int32, here.shape, 1)
+
+    def at(k):
+        if k == 0:
+            return here
+        return turn(jnp.where(lane < k if k > 0 else lane >= LANE + k, there, here), -k, 1)
+
+    return at
+
+
+def ahead_at(at):
+    return (at(1) - at(0)) + ratio * (at(2) - at(-1))
+
+
+def behind_at(at):
+    return (at(0) - at(-1)) + ratio * (at(1) - at(-2))
+
+
 def advance(
     forward_ref,
     adjoint_ref,
@@ -290,7 +309,9 @@
                 ahead(get(SXZ), 0) + ahead(get(SYZ), 1),
             )
             for i, change in enumerate(changes):
-                speed_ref[3 * state + i, z] = get(i) + scaled * change
+                speed = get(i) + scaled * change
+                speed_ref[3 * state + i, z, :, :LANE] = speed[:, :LANE]
+                speed_ref[3 * state + i, z, :rows, LANE:] = speed[:rows, LANE:]
 
     for z in range(depth):
         rates = []
@@ -299,15 +320,19 @@
                 lambda k: speed_ref[base + i, k, :rows, :LANE], z, depth, offset
             )
             over_x = lambda i, way: way(speed_ref[base + i, z, :, :LANE], 0)[:rows]
-            over_y = lambda i, way: way(speed_ref[base + i, z, :rows, :], 1)[:, :LANE]
+            over_y = lambda i, way: way(
+                crossing(
+                    speed_ref[base + i, z, :rows, :LANE], speed_ref[base + i, z, :rows, LANE:]
+                )
+            )
             rates.append(
                 (
                     over_x(0, ahead),
-                    over_y(1, ahead),
+                    over_y(1, ahead_at),
                     along(2, 0),
-                    over_y(0, behind) + over_x(1, behind),
+                    over_y(0, behind_at) + over_x(1, behind),
                     along(0, -1) + over_x(2, behind),
-                    along(1, -1) + over_y(2, behind),
+                    along(1, -1) + over_y(2, behind_at),
                 )
             )
         one, two = rates

time: 42.2 us -> 42 us (level)
  no operation moved by 1% of the time
where the time goes in v4:
time: 42 us; the launch traced here: 41.8 us
  starting transfers between devices  15.8 us (38%)
  blocking collectives  12 us (29%)
  waiting for transfers between devices  9.28 us (22%)
  Pallas kernels  3.27 us (8%)
  between operations  0.74 us (2%)
  other arithmetic  0.67 us (2%)
    all_to_all x1, blocking collectives, shards(): lax.all_to_all(pairs, 'ev', 0, 0, axis_index_groups=groups, tiled=True)  12 us
    ppermute x2, starting transfers between devices, exchange(): lax.ppermute(first, axis, swaps(devices, 0))  8.59 us
    ppermute x2, waiting for transfers between devices, exchange(): lax.ppermute(second, axis, swaps(devices, 1))  5.05 us
    ppermute x1, starting transfers between devices, shards(): partner = lax.ppermute(terms, 'ev', [(i, i ^ 1) for i in range(events)])  4.64 us
    pallas_call x6, Pallas kernels, on_chip(): pl.pallas_call(kernel, out_shape=[(pltpu.HBM if k in away else pltpu.VMEM...  3.27 us
    ppermute x1, waiting for transfers between devices, shards(): partner = lax.ppermute(terms, 'ev', [(i, i ^ 1) for i in range(events)])  3.02 us
    ppermute x2, starting transfers between devices, exchange(): lax.ppermute(second, axis, swaps(devices, 1))  2.58 us
    ppermute x2, waiting for transfers between devices, exchange(): lax.ppermute(first, axis, swaps(devices, 0))  1.22 us
  transfers between devices with their start and end apart: 5, of which 4 were waited for; matrix products, arithmetic and copies ran while one was open for 0% of the time, Pallas kernels for 2%

profile of v4, /device:TPU:128, one launch (start us, length us, event | category | flops | bytes accessed | tf_op | source)
XLA Modules:
  0.0 41.8 jit_solution(6124905296556808113)
XLA Ops:
  0.6 1.2 %shard_map.95 = (f32[20,8,128]{2,1,0:T(8,128)S(1)}, f32[20,8,128]{2,1,0:T(8,128)S(1)}, f32[6,4,16,128]{3,2,1,0:T(8,128)S(1)}, f32[1,9,4,16,128]{4,3,2,1,0:T(8,12...) custom-call(f32[1,9,4,16,128]{4,3,2,1,0:T(8,128)} %forward_hbm.1, ...), custom_call_target="tpu_custom_call" | custom-call | flops 2000000 | bytes 2000000 | tf_op jit(solution)/shard_map/pallas_call | solution.py:385
  1.9 3.8 %collective-permute-start = (f32[20,8,128]{2,1,0:T(8,128)S(1)}, f32[20,8,128]{2,1,0:T(8,128)S(1)}, u32[]{:S(2)}, u32[]{:S(2)}) collective-permute-start(f32[20,8,128]{2,1,0:T(8,128)S(1)} %get-tuple-element.17), channel_id=1, source_target_pairs={{0,4},{8,12},{16,20},{24,28},{32,36},{40,44},{48,52},{56,60},{4,0}... | collective-permute-start | bytes 245768 | tf_op jit(solution)/shard_map/ppermute | solution.py:407
  5.7 1.9 %collective-permute-start.1 = (f32[20,8,128]{2,1,0:T(8,128)S(1)}, f32[20,8,128]{2,1,0:T(8,128)S(1)}, u32[]{:S(2)}, u32[]{:S(2)}) collective-permute-start(f32[20,8,128]{2,1,0:T(8,128)S(1)} %get-tuple-element.18), channel_id=1, source_target_pairs={{4,8},{12,16},{20,24},{28,32},{36,40},{44,48},{52,56},{8,4},{16,12... | collective-permute-start | bytes 245768 | tf_op jit(solution)/shard_map/ppermute | solution.py:408
  7.6 0.2 shard_map.96.own_ref
  7.8 0.4 collective-permute-done.first_ref
  8.2 5.0 %collective-permute-done.1.second_ref = f32[20,8,128]{2,1,0:T(8,128)S(1)} collective-permute-done((f32[20,8,128]{2,1,0:T(8,128)S(1)}, f32[20,8,128]{2,1,0:T(8,128)S(1)}, u32[]{:S(2)}, u32[]{:S(2)}) %collective-permute-start.1) | collective-permute-done | bytes 81952 | tf_op jit(solution)/shard_map/ppermute | solution.py:408
  13.3 0.1 shard_map.97
  13.4 0.7 %collective-permute-start.3 = (f32[4,24,128]{2,1,0:T(8,128)S(1)}, f32[4,24,128]{2,1,0:T(8,128)S(1)}, u32[]{:S(2)}, u32[]{:S(2)}) collective-permute-start(f32[4,24,128]{2,1,0:T(8,128)S(1)} %get-tuple-element.20), channel_id=1, source_target_pairs={{1,2},{2,1},{5,6},{6,5},{9,10},{10,9},{13,14},{14,13},{17,18},{18,... | collective-permute-start | bytes 147464 | tf_op jit(solution)/shard_map/ppermute | solution.py:408
  14.1 4.8 %collective-permute-start.2 = (f32[4,24,128]{2,1,0:T(8,128)S(1)}, f32[4,24,128]{2,1,0:T(8,128)S(1)}, u32[]{:S(2)}, u32[]{:S(2)}) collective-permute-start(f32[4,24,128]{2,1,0:T(8,128)S(1)} %get-tuple-element.20), channel_id=1, source_target_pairs={{0,1},{2,3},{1,0},{3,2},{4,5},{6,7},{5,4},{7,6},{8,9},{10,11},{9,8... | collective-permute-start | bytes 147464 | tf_op jit(solution)/shard_map/ppermute | solution.py:407
  18.8 0.0 collective-permute-done.3.second_ref
  18.8 0.8 %collective-permute-done.2.first_ref = f32[4,24,128]{2,1,0:T(8,128)S(1)} collective-permute-done((f32[4,24,128]{2,1,0:T(8,128)S(1)}, f32[4,24,128]{2,1,0:T(8,128)S(1)}, u32[]{:S(2)}, u32[]{:S(2)}) %collective-permute-start.2) | collective-permute-done | bytes 49184 | tf_op jit(solution)/shard_map/ppermute | solution.py:407
  19.7 0.0 copy-start
  19.7 0.0 copy-start.1
  19.7 0.9 %shard_map.98 = (f32[3,4,16,128]{3,2,1,0:T(8,128)S(1)}, f32[3,4,16,128]{3,2,1,0:T(8,128)S(1)}, f32[6,4,16,128]{3,2,1,0:T(8,128)S(1)}) custom-call(f32[1,9,4,16,128]{4,3,2,1,0:T(8,128)S(1)} %get-tuple-element.13.forward_ref, f32[1,9,4,16,128]{4,3,2,1,0:T(8,128)S(1)} %get-tuple-element.14.adjoint_ref, f32[6,4,16,128]{3,2,1,0:T(8,128)S(1)} %get-tuple-element.15.pushed_ref, ...), custom_call_target="tpu_custom_call" | custom-call | flops 4000000 | bytes 4000000 | tf_op jit(solution)/shard_map/pallas_call | solution.py:385
  20.6 4.6 %collective-permute-start.4 = (f32[3,4,16,128]{3,2,1,0:T(8,128)S(1)}, f32[3,4,16,128]{3,2,1,0:T(8,128)S(1)}, u32[]{:S(2)}, u32[]{:S(2)}) collective-permute-start(f32[3,4,16,128]{3,2,1,0:T(8,128)S(1)} %get-tuple-element.23.one_ref), channel_id=1, source_target_pairs={{0,64},{64,0},{128,192},{192,128},{256,320},{320,256},{384,448},{4... | collective-permute-start | bytes 294920 | tf_op jit(solution)/shard_map/ppermute | solution.py:460
  25.3 0.0 copy-done
  25.3 0.0 copy-done.1
  25.3 0.8 %shard_map.99._ = f32[1,9,4,16,128]{4,3,2,1,0:T(8,128)} custom-call(f32[1,9,4,16,128]{4,3,2,1,0:T(8,128)S(1)} %get-tuple-element.13.forward_ref, f32[4,16,128]{2,1,0:T(8,128)S(1)} %copy-done, f32[4,16,128]{2,1,0:T(8,128)S(1)} %copy-done.1, f32[3,4,16,128]{3,2,1,0:T(8,128)S(1)} %get-tuple-element.21.moved_ref, f32[6,4,16,128]{3,2,1,0:T(8,128)S(1)} %get-tuple-element.22.rates_ref), custom_call_target="tpu_custom_call" | custom-call | flops 2000000 | bytes 2000000 | tf_op jit(solution)/shard_map/pallas_call | solution.py:385
  26.1 3.0 %collective-permute-done.4.two_ref = f32[3,4,16,128]{3,2,1,0:T(8,128)S(1)} collective-permute-done((f32[3,4,16,128]{3,2,1,0:T(8,128)S(1)}, f32[3,4,16,128]{3,2,1,0:T(8,128)S(1)}, u32[]{:S(2)}, u32[]{:S(2)}) %collective-permute-start.4) | collective-permute-done | bytes 98336 | tf_op jit(solution)/shard_map/ppermute | solution.py:460
  29.1 12.0 %all_to_all.5 = f32[4,3,4,16,128]{4,3,2,1,0:T(8,128)S(1)} all-to-all(f32[4,3,4,16,128]{4,3,2,1,0:T(8,128)S(1)} %shard_map.100), channel_id=1, replica_groups={{0,128,256,384},{64,192,320,448},{1,129,257,385},{65,193,321,449},{2,13..., dimensions={0} | all-to-all | bytes 786432 | tf_op jit(solution)/shard_map/all_to_all | solution.py:475
  41.1 0.7 %reduce_sum.9 = f32[3,4,16,128]{3,2,1,0:T(8,128)} reduce(f32[4,3,4,16,128]{4,3,2,1,0:T(8,128)S(1)} %all_to_all.5, f32[]{:T(128)} %constant.0.clone.1), dimensions={0}, to_apply=%region_0.0 | reduce | flops 73728 | bytes 491524 | tf_op jit(solution)/shard_map/reduce_sum | solution.py:474
  (1 shorter events, 0.0 us)
Async XLA Ops:
  1.9 6.3 %collective-permute-start = (f32[20,8,128]{2,1,0:T(8,128)S(1)}, f32[20,8,128]{2,1,0:T(8,128)S(1)}, u32[]{:S(2)}, u32[]{:S(2)}) collective-permute-start(f32[20,8,128]{2,1,0:T(8,128)S(1)} %get-tuple-element.17), channel_id=1, source_target_pairs={{0,4},{8,12},{16,20},{24,28},{32,36},{40,44},{48,52},{56,60},{4,0}... | collective-permute-start | bytes 245768 | tf_op jit(solution)/shard_map/ppermute | solution.py:407
  5.7 7.5 %collective-permute-start.1 = (f32[20,8,128]{2,1,0:T(8,128)S(1)}, f32[20,8,128]{2,1,0:T(8,128)S(1)}, u32[]{:S(2)}, u32[]{:S(2)}) collective-permute-start(f32[20,8,128]{2,1,0:T(8,128)S(1)} %get-tuple-element.18), channel_id=1, source_target_pairs={{4,8},{12,16},{20,24},{28,32},{36,40},{44,48},{52,56},{8,4},{16,12... | collective-permute-start | bytes 245768 | tf_op jit(solution)/shard_map/ppermute | solution.py:408
  13.4 5.4 %collective-permute-start.3 = (f32[4,24,128]{2,1,0:T(8,128)S(1)}, f32[4,24,128]{2,1,0:T(8,128)S(1)}, u32[]{:S(2)}, u32[]{:S(2)}) collective-permute-start(f32[4,24,128]{2,1,0:T(8,128)S(1)} %get-tuple-element.20), channel_id=1, source_target_pairs={{1,2},{2,1},{5,6},{6,5},{9,10},{10,9},{13,14},{14,13},{17,18},{18,... | collective-permute-start | bytes 147464 | tf_op jit(solution)/shard_map/ppermute | solution.py:408
  14.1 5.6 %collective-permute-start.2 = (f32[4,24,128]{2,1,0:T(8,128)S(1)}, f32[4,24,128]{2,1,0:T(8,128)S(1)}, u32[]{:S(2)}, u32[]{:S(2)}) collective-permute-start(f32[4,24,128]{2,1,0:T(8,128)S(1)} %get-tuple-element.20), channel_id=1, source_target_pairs={{0,1},{2,3},{1,0},{3,2},{4,5},{6,7},{5,4},{7,6},{8,9},{10,11},{9,8... | collective-permute-start | bytes 147464 | tf_op jit(solution)/shard_map/ppermute | solution.py:407
  19.7 5.6 %copy-start = (f32[4,16,128]{2,1,0:T(8,128)S(1)}, f32[4,16,128]{2,1,0:T(8,128)}, u32[]{:S(2)}) copy-start(f32[4,16,128]{2,1,0:T(8,128)} %lame_ref.1) | copy-start | bytes 98308
  19.7 5.6 %copy-start.1 = (f32[4,16,128]{2,1,0:T(8,128)S(1)}, f32[4,16,128]{2,1,0:T(8,128)}, u32[]{:S(2)}) copy-start(f32[4,16,128]{2,1,0:T(8,128)} %shear_ref.1) | copy-start | bytes 98308
  20.6 8.4 %collective-permute-start.4 = (f32[3,4,16,128]{3,2,1,0:T(8,128)S(1)}, f32[3,4,16,128]{3,2,1,0:T(8,128)S(1)}, u32[]{:S(2)}, u32[]{:S(2)}) collective-permute-start(f32[3,4,16,128]{3,2,1,0:T(8,128)S(1)} %get-tuple-element.23.one_ref), channel_id=1, source_target_pairs={{0,64},{64,0},{128,192},{192,128},{256,320},{320,256},{384,448},{4... | collective-permute-start | bytes 294920 | tf_op jit(solution)/shard_map/ppermute | solution.py:460

commit v5 on v4

--- a/solution.py
+++ b/solution.py
@@ -302,16 +302,19 @@
         for z in range(depth):
             get = lambda field: field_ref[state * ADJOINT + field, z]
             scaled = (step * inner_coeff) * field_ref[BUOYANCY, z]
-            sxy = get(SXY)
-            changes = (
-                behind(get(SXX), 0) + ahead(sxy, 1),
-                ahead(sxy, 0) + behind(get(SYY), 1),
-                ahead(get(SXZ), 0) + ahead(get(SYZ), 1),
-            )
-            for i, change in enumerate(changes):
-                speed = get(i) + scaled * change
-                speed_ref[3 * state + i, z, :, :LANE] = speed[:, :LANE]
-                speed_ref[3 * state + i, z, :rows, LANE:] = speed[:rows, LANE:]
+            ways = ((SXX, behind, SXY, ahead), (SXY, ahead, SYY, behind), (SXZ, ahead, SYZ, ahead))
+            for i, (tall, way_x, wide, way_y) in enumerate(ways):
+                over_x = way_x(get(tall), 0)
+                across, push = get(wide), get(i)
+                over_y = way_y(across[:rows], 1)
+                speed_ref[3 * state + i, z, :rows, :] = push[:rows] + scaled[:rows] * (
+                    over_x[:rows] + over_y
+                )
+                edge_way = ahead_at if way_y is ahead else behind_at
+                over_y = edge_way(crossing(across[rows:, :LANE], across[rows:, LANE:]))
+                speed_ref[3 * state + i, z, rows:, :LANE] = push[rows:, :LANE] + scaled[
+                    rows:, :LANE
+                ] * (over_x[rows:, :LANE] + over_y)
 
     for z in range(depth):
         rates = []

time: 42 us -> 42 us (level)
  no operation moved by 1% of the time
where the time goes in v5:
time: 42 us; the launch traced here: 41.7 us
  starting transfers between devices  15.8 us (38%)
  blocking collectives  12 us (29%)
  waiting for transfers between devices  9.28 us (22%)
  Pallas kernels  3.2 us (8%)
  between operations  0.74 us (2%)
  other arithmetic  0.67 us (2%)
    all_to_all x1, blocking collectives, shards(): lax.all_to_all(pairs, 'ev', 0, 0, axis_index_groups=groups, tiled=True)  12 us
    ppermute x2, starting transfers between devices, exchange(): lax.ppermute(first, axis, swaps(devices, 0))  8.59 us
    ppermute x2, waiting for transfers between devices, exchange(): lax.ppermute(second, axis, swaps(devices, 1))  5.05 us
    ppermute x1, starting transfers between devices, shards(): partner = lax.ppermute(terms, 'ev', [(i, i ^ 1) for i in range(events)])  4.64 us
    pallas_call x6, Pallas kernels, on_chip(): pl.pallas_call(kernel, out_shape=[(pltpu.HBM if k in away else pltpu.VMEM...  3.2 us
    ppermute x1, waiting for transfers between devices, shards(): partner = lax.ppermute(terms, 'ev', [(i, i ^ 1) for i in range(events)])  3.02 us
    ppermute x2, starting transfers between devices, exchange(): lax.ppermute(second, axis, swaps(devices, 1))  2.58 us
    ppermute x2, waiting for transfers between devices, exchange(): lax.ppermute(first, axis, swaps(devices, 0))  1.22 us
  transfers between devices with their start and end apart: 5, of which 4 were waited for; matrix products, arithmetic and copies ran while one was open for 0% of the time, Pallas kernels for 2%

profile of v5, /device:TPU:128, one launch (start us, length us, event | category | flops | bytes accessed | tf_op | source)
XLA Modules:
  0.0 41.7 jit_solution(8308801037237118887)
XLA Ops:
  0.6 1.2 %shard_map.95 = (f32[20,8,128]{2,1,0:T(8,128)S(1)}, f32[20,8,128]{2,1,0:T(8,128)S(1)}, f32[6,4,16,128]{3,2,1,0:T(8,128)S(1)}, f32[1,9,4,16,128]{4,3,2,1,0:T(8,12...) custom-call(f32[1,9,4,16,128]{4,3,2,1,0:T(8,128)} %forward_hbm.1, ...), custom_call_target="tpu_custom_call" | custom-call | flops 2000000 | bytes 2000000 | tf_op jit(solution)/shard_map/pallas_call | solution.py:388
  1.9 3.8 %collective-permute-start = (f32[20,8,128]{2,1,0:T(8,128)S(1)}, f32[20,8,128]{2,1,0:T(8,128)S(1)}, u32[]{:S(2)}, u32[]{:S(2)}) collective-permute-start(f32[20,8,128]{2,1,0:T(8,128)S(1)} %get-tuple-element.17), channel_id=1, source_target_pairs={{0,4},{8,12},{16,20},{24,28},{32,36},{40,44},{48,52},{56,60},{4,0}... | collective-permute-start | bytes 245768 | tf_op jit(solution)/shard_map/ppermute | solution.py:410
  5.7 1.9 %collective-permute-start.1 = (f32[20,8,128]{2,1,0:T(8,128)S(1)}, f32[20,8,128]{2,1,0:T(8,128)S(1)}, u32[]{:S(2)}, u32[]{:S(2)}) collective-permute-start(f32[20,8,128]{2,1,0:T(8,128)S(1)} %get-tuple-element.18), channel_id=1, source_target_pairs={{4,8},{12,16},{20,24},{28,32},{36,40},{44,48},{52,56},{8,4},{16,12... | collective-permute-start | bytes 245768 | tf_op jit(solution)/shard_map/ppermute | solution.py:411
  7.6 0.2 shard_map.96.own_ref
  7.8 0.4 collective-permute-done.first_ref
  8.2 5.0 %collective-permute-done.1.second_ref = f32[20,8,128]{2,1,0:T(8,128)S(1)} collective-permute-done((f32[20,8,128]{2,1,0:T(8,128)S(1)}, f32[20,8,128]{2,1,0:T(8,128)S(1)}, u32[]{:S(2)}, u32[]{:S(2)}) %collective-permute-start.1) | collective-permute-done | bytes 81952 | tf_op jit(solution)/shard_map/ppermute | solution.py:411
  13.3 0.1 shard_map.97
  13.4 0.7 %collective-permute-start.3 = (f32[4,24,128]{2,1,0:T(8,128)S(1)}, f32[4,24,128]{2,1,0:T(8,128)S(1)}, u32[]{:S(2)}, u32[]{:S(2)}) collective-permute-start(f32[4,24,128]{2,1,0:T(8,128)S(1)} %get-tuple-element.20), channel_id=1, source_target_pairs={{1,2},{2,1},{5,6},{6,5},{9,10},{10,9},{13,14},{14,13},{17,18},{18,... | collective-permute-start | bytes 147464 | tf_op jit(solution)/shard_map/ppermute | solution.py:411
  14.1 4.8 %collective-permute-start.2 = (f32[4,24,128]{2,1,0:T(8,128)S(1)}, f32[4,24,128]{2,1,0:T(8,128)S(1)}, u32[]{:S(2)}, u32[]{:S(2)}) collective-permute-start(f32[4,24,128]{2,1,0:T(8,128)S(1)} %get-tuple-element.20), channel_id=1, source_target_pairs={{0,1},{2,3},{1,0},{3,2},{4,5},{6,7},{5,4},{7,6},{8,9},{10,11},{9,8... | collective-permute-start | bytes 147464 | tf_op jit(solution)/shard_map/ppermute | solution.py:410
  18.8 0.0 collective-permute-done.3.second_ref
  18.8 0.8 %collective-permute-done.2.first_ref = f32[4,24,128]{2,1,0:T(8,128)S(1)} collective-permute-done((f32[4,24,128]{2,1,0:T(8,128)S(1)}, f32[4,24,128]{2,1,0:T(8,128)S(1)}, u32[]{:S(2)}, u32[]{:S(2)}) %collective-permute-start.2) | collective-permute-done | bytes 49184 | tf_op jit(solution)/shard_map/ppermute | solution.py:410
  19.7 0.0 copy-start
  19.7 0.0 copy-start.1
  19.7 0.8 %shard_map.98 = (f32[3,4,16,128]{3,2,1,0:T(8,128)S(1)}, f32[3,4,16,128]{3,2,1,0:T(8,128)S(1)}, f32[6,4,16,128]{3,2,1,0:T(8,128)S(1)}) custom-call(f32[1,9,4,16,128]{4,3,2,1,0:T(8,128)S(1)} %get-tuple-element.13.forward_ref, f32[1,9,4,16,128]{4,3,2,1,0:T(8,128)S(1)} %get-tuple-element.14.adjoint_ref, f32[6,4,16,128]{3,2,1,0:T(8,128)S(1)} %get-tuple-element.15.pushed_ref, ...), custom_call_target="tpu_custom_call" | custom-call | flops 4000000 | bytes 4000000 | tf_op jit(solution)/shard_map/pallas_call | solution.py:388
  20.6 4.6 %collective-permute-start.4 = (f32[3,4,16,128]{3,2,1,0:T(8,128)S(1)}, f32[3,4,16,128]{3,2,1,0:T(8,128)S(1)}, u32[]{:S(2)}, u32[]{:S(2)}) collective-permute-start(f32[3,4,16,128]{3,2,1,0:T(8,128)S(1)} %get-tuple-element.23.one_ref), channel_id=1, source_target_pairs={{0,64},{64,0},{128,192},{192,128},{256,320},{320,256},{384,448},{4... | collective-permute-start | bytes 294920 | tf_op jit(solution)/shard_map/ppermute | solution.py:463
  25.2 0.0 copy-done
  25.2 0.0 copy-done.1
  25.2 0.8 %shard_map.99._ = f32[1,9,4,16,128]{4,3,2,1,0:T(8,128)} custom-call(f32[1,9,4,16,128]{4,3,2,1,0:T(8,128)S(1)} %get-tuple-element.13.forward_ref, f32[4,16,128]{2,1,0:T(8,128)S(1)} %copy-done, f32[4,16,128]{2,1,0:T(8,128)S(1)} %copy-done.1, f32[3,4,16,128]{3,2,1,0:T(8,128)S(1)} %get-tuple-element.21.moved_ref, f32[6,4,16,128]{3,2,1,0:T(8,128)S(1)} %get-tuple-element.22.rates_ref), custom_call_target="tpu_custom_call" | custom-call | flops 2000000 | bytes 2000000 | tf_op jit(solution)/shard_map/pallas_call | solution.py:388
  26.0 3.0 %collective-permute-done.4.two_ref = f32[3,4,16,128]{3,2,1,0:T(8,128)S(1)} collective-permute-done((f32[3,4,16,128]{3,2,1,0:T(8,128)S(1)}, f32[3,4,16,128]{3,2,1,0:T(8,128)S(1)}, u32[]{:S(2)}, u32[]{:S(2)}) %collective-permute-start.4) | collective-permute-done | bytes 98336 | tf_op jit(solution)/shard_map/ppermute | solution.py:463
  29.0 12.0 %all_to_all.5 = f32[4,3,4,16,128]{4,3,2,1,0:T(8,128)S(1)} all-to-all(f32[4,3,4,16,128]{4,3,2,1,0:T(8,128)S(1)} %shard_map.100), channel_id=1, replica_groups={{0,128,256,384},{64,192,320,448},{1,129,257,385},{65,193,321,449},{2,13..., dimensions={0} | all-to-all | bytes 786432 | tf_op jit(solution)/shard_map/all_to_all | solution.py:478
  41.0 0.7 %reduce_sum.9 = f32[3,4,16,128]{3,2,1,0:T(8,128)} reduce(f32[4,3,4,16,128]{4,3,2,1,0:T(8,128)S(1)} %all_to_all.5, f32[]{:T(128)} %constant.0.clone.1), dimensions={0}, to_apply=%region_0.0 | reduce | flops 73728 | bytes 491524 | tf_op jit(solution)/shard_map/reduce_sum | solution.py:477
  (1 shorter events, 0.0 us)
Async XLA Ops:
  1.9 6.3 %collective-permute-start = (f32[20,8,128]{2,1,0:T(8,128)S(1)}, f32[20,8,128]{2,1,0:T(8,128)S(1)}, u32[]{:S(2)}, u32[]{:S(2)}) collective-permute-start(f32[20,8,128]{2,1,0:T(8,128)S(1)} %get-tuple-element.17), channel_id=1, source_target_pairs={{0,4},{8,12},{16,20},{24,28},{32,36},{40,44},{48,52},{56,60},{4,0}... | collective-permute-start | bytes 245768 | tf_op jit(solution)/shard_map/ppermute | solution.py:410
  5.7 7.5 %collective-permute-start.1 = (f32[20,8,128]{2,1,0:T(8,128)S(1)}, f32[20,8,128]{2,1,0:T(8,128)S(1)}, u32[]{:S(2)}, u32[]{:S(2)}) collective-permute-start(f32[20,8,128]{2,1,0:T(8,128)S(1)} %get-tuple-element.18), channel_id=1, source_target_pairs={{4,8},{12,16},{20,24},{28,32},{36,40},{44,48},{52,56},{8,4},{16,12... | collective-permute-start | bytes 245768 | tf_op jit(solution)/shard_map/ppermute | solution.py:411
  13.4 5.4 %collective-permute-start.3 = (f32[4,24,128]{2,1,0:T(8,128)S(1)}, f32[4,24,128]{2,1,0:T(8,128)S(1)}, u32[]{:S(2)}, u32[]{:S(2)}) collective-permute-start(f32[4,24,128]{2,1,0:T(8,128)S(1)} %get-tuple-element.20), channel_id=1, source_target_pairs={{1,2},{2,1},{5,6},{6,5},{9,10},{10,9},{13,14},{14,13},{17,18},{18,... | collective-permute-start | bytes 147464 | tf_op jit(solution)/shard_map/ppermute | solution.py:411
  14.1 5.6 %collective-permute-start.2 = (f32[4,24,128]{2,1,0:T(8,128)S(1)}, f32[4,24,128]{2,1,0:T(8,128)S(1)}, u32[]{:S(2)}, u32[]{:S(2)}) collective-permute-start(f32[4,24,128]{2,1,0:T(8,128)S(1)} %get-tuple-element.20), channel_id=1, source_target_pairs={{0,1},{2,3},{1,0},{3,2},{4,5},{6,7},{5,4},{7,6},{8,9},{10,11},{9,8... | collective-permute-start | bytes 147464 | tf_op jit(solution)/shard_map/ppermute | solution.py:410
  19.7 5.5 %copy-start = (f32[4,16,128]{2,1,0:T(8,128)S(1)}, f32[4,16,128]{2,1,0:T(8,128)}, u32[]{:S(2)}) copy-start(f32[4,16,128]{2,1,0:T(8,128)} %lame_ref.1) | copy-start | bytes 98308
  19.7 5.5 %copy-start.1 = (f32[4,16,128]{2,1,0:T(8,128)S(1)}, f32[4,16,128]{2,1,0:T(8,128)}, u32[]{:S(2)}) copy-start(f32[4,16,128]{2,1,0:T(8,128)} %shear_ref.1) | copy-start | bytes 98308
  20.6 8.4 %collective-permute-start.4 = (f32[3,4,16,128]{3,2,1,0:T(8,128)S(1)}, f32[3,4,16,128]{3,2,1,0:T(8,128)S(1)}, u32[]{:S(2)}, u32[]{:S(2)}) collective-permute-start(f32[3,4,16,128]{3,2,1,0:T(8,128)S(1)} %get-tuple-element.23.one_ref), channel_id=1, source_target_pairs={{0,64},{64,0},{128,192},{192,128},{256,320},{320,256},{384,448},{4... | collective-permute-start | bytes 294920 | tf_op jit(solution)/shard_map/ppermute | solution.py:463
